TPU v7x, 256 devices: a whole 4x4x8 slice. The times are simulated.
256 devices in a mesh: dp: 16 (over y_hi, x, core), seq: 16 (over y_lo, z).
Axes of the slice: x: 4, y: 4 (y_hi: 2, y_lo: 2; y = y_hi * 2 + y_lo), z: 8, core: 2. Of those that a mesh axis runs over, the one named last changes fastest.
Arguments:
- queries: bfloat16 [16, 2048, 4096], P('dp', 'seq'), may hold values from -512 to 512
- key_rows: bfloat16 [16, 2048, 4096], P('dp', 'seq'), may hold values from -18 to 18
- value_rows: bfloat16 [16, 2048, 4096], P('dp', 'seq'), may hold values from -6 to 6
- w_out: bfloat16 [4096, 3072], P('seq', 'dp'), may hold values from -1.5 to 1.5
Outputs:
- attn_output: bfloat16 [16, 2048, 3072], P('dp', 'seq')
All inputs are finite; a program needn't handle non-finite values.
Results may differ from a plain program's by a relative error of at most 0.0095.
Values may be sent and summed in bfloat16 or wider, within the bound.
No kernel may reach another device: no remote copies, remote signals or barrier semaphores. Data moves between devices by JAX's collectives and lax.ppermute only.
A program may use at most 128 MiB of HBM per device.

v0:
```python
import functools

import jax
import jax.numpy as jnp
import numpy as np
from jax import lax
from jax.experimental import pallas as pl
from jax.experimental.pallas import tpu as pltpu
from jax.sharding import Mesh
from jax.sharding import PartitionSpec as P

HEAD_DIM = 128
SCALE = float(np.log2(np.e) / np.sqrt(HEAD_DIM))
DP = ("yh", "x", "core")
SEQ = ("yl", "z")
BF16 = jnp.bfloat16
F32 = jnp.float32


def cost(flops, nbytes, exps=0):
    return pl.CostEstimate(flops=flops, bytes_accessed=nbytes, transcendentals=exps)


def pack_kernel(head, q_ref, k_ref, v_ref, out_ref):
    for index, ref in enumerate((q_ref, k_ref, v_ref)):
        for group in range(out_ref.shape[0]):
            low = group * 256 + head * HEAD_DIM
            out_ref[group, index] = ref[:, low : low + HEAD_DIM]


def pack(queries, key_rows, value_rows, head):
    tokens = queries.shape[0]
    spec = pl.BlockSpec((tokens, 1024), lambda i: (0, i))
    return pl.pallas_call(
        functools.partial(pack_kernel, head),
        grid=(4,),
        in_specs=[spec] * 3,
        out_specs=pl.BlockSpec((4, 3, tokens, HEAD_DIM), lambda i: (i, 0, 0, 0)),
        out_shape=jax.ShapeDtypeStruct((16, 3, tokens, HEAD_DIM), BF16),
        cost_estimate=cost(0, 5 << 20),
    )(queries, key_rows, value_rows)


def attend_kernel(sub, q_ref, k_ref, v_ref, o_ref):
    keys = k_ref[:, 0].reshape(-1, HEAD_DIM)
    values = v_ref[:, 0].reshape(-1, HEAD_DIM)
    rows = q_ref[:, 0].reshape(-1, HEAD_DIM)
    pieces = []
    for low in range(0, rows.shape[0], sub):
        scores = lax.dot_general(
            rows[low : low + sub], keys, (((1,), (1,)), ((), ())), preferred_element_type=F32
        )
        largest = jnp.max(scores, axis=1, keepdims=True)
        weights = jnp.exp2((scores - largest) * SCALE)
        total = jnp.sum(weights, axis=1, keepdims=True)
        mixed = jnp.dot(weights.astype(BF16), values, preferred_element_type=F32)
        pieces.append((mixed / total).astype(BF16))
    o_ref[...] = jnp.concatenate(pieces, 0).reshape(o_ref.shape)


def attend(arrived):
    n, _, tokens, _ = arrived.shape
    per = 4
    return pl.pallas_call(
        functools.partial(attend_kernel, 256),
        grid=(n // per,),
        in_specs=[
            pl.BlockSpec((per, 1, tokens, HEAD_DIM), lambda i: (i, 0, 0, 0)),
            pl.BlockSpec((n, 1, tokens, HEAD_DIM), lambda i: (0, 1, 0, 0)),
            pl.BlockSpec((n, 1, tokens, HEAD_DIM), lambda i: (0, 2, 0, 0)),
        ],
        out_specs=pl.BlockSpec((per, tokens, HEAD_DIM), lambda i: (i, 0, 0)),
        out_shape=jax.ShapeDtypeStruct((n, tokens, HEAD_DIM), BF16),
        compiler_params=pltpu.CompilerParams(vmem_limit_bytes=48 << 20),
        cost_estimate=cost(4 * 2048 * 2048 * 128, 2 << 20, 2048 * 2048),
    )(arrived, arrived, arrived)


NEAR = (0, -1, 1, -2, 2)
FAR = (-3, 3, -4)
Z_OFFSETS = NEAR + FAR
X_OFFSETS = (0, -1, 1, 2)
ROWS_A, ROWS_B = 80, 112


def gather_features(pos_ref, a_ref, b_ref, a_rel):
    tokens = a_ref.shape[1]
    yl, z = pos_ref[1], pos_ref[2]
    for half in range(2):
        group_y = yl if half == 0 else 1 - yl
        for i, offset in enumerate(Z_OFFSETS):
            group = group_y * 8 + lax.rem(z + (8 + offset), 8)
            low = (half * 8 + i) * HEAD_DIM
            a_rel[:tokens, low : low + HEAD_DIM] = a_ref[group]
            a_rel[tokens:, low : low + HEAD_DIM] = b_ref[group]


def weight_rows(groups, same):
    columns = []
    for half in range(2):
        for own, pair, cross, far, x0, x1, x2, x3a, x3b in groups:
            part_a = ((own, pair) if same else (far, cross))[half]
            y = ((0, 1) if same else (3, 2))[half]
            part_x3 = (x3a, x3b)[y // 2]
            for i in range(own.shape[1]):
                rows = [part_a[:, i].reshape(4 * ROWS_A, HEAD_DIM)]
                rows += [x0[y, i], x1[y, i], x2[y, i], part_x3[y % 2, i]]
                columns.append(jnp.concatenate(rows, axis=0))
    return jnp.concatenate(columns, axis=1)


def project_kernel(head, pos_ref, a_ref, b_ref, *refs):
    groups = (refs[:9], refs[9:18])
    a_rel = refs[-1]
    gather_features(pos_ref, a_ref, b_ref, a_rel)
    tokens = a_ref.shape[1]
    for same in (True, False):
        yh = pos_ref[0] if same else 1 - pos_ref[0]
        total = lax.dot_general(
            weight_rows(groups, same),
            a_rel[...],
            (((1,), (1,)), ((), ())),
            preferred_element_type=F32,
        )
        for j, offset in enumerate(X_OFFSETS):
            x = lax.rem(pos_ref[3] + (4 + offset), 4)
            first = 4 * ROWS_A + j * ROWS_B
            parts = (
                (0, ROWS_A, total[j * ROWS_A : (j + 1) * ROWS_A]),
                (ROWS_A, 192, total[first : first + ROWS_B]),
            )
            for low, high, part in parts:
                if head == 0:
                    refs[18][yh, x, low:high] = part
                else:
                    part = part + refs[18][yh, x, low:high]
                    refs[19][yh, x, low:high] = part[:, :tokens].astype(BF16)
                    refs[20][yh, x, low:high] = part[:, tokens:].astype(BF16)


def project(pos, a, b, groups, head, acc=None):
    tokens = a.shape[1]
    whole = pl.BlockSpec(memory_space=pltpu.VMEM)
    buffers = [buffer for group in groups for buffer in group]

    def half(buffer):
        return pl.BlockSpec((*buffer.shape[:3], HEAD_DIM), lambda i, p: (0, 0, 0, head))

    if head == 0:
        shapes = jax.ShapeDtypeStruct((2, 4, 192, 2 * tokens), F32)
        out_specs, extra = whole, []
    else:
        shapes = [jax.ShapeDtypeStruct((2, 4, 192, tokens), BF16)] * 2
        out_specs, extra = [whole, whole], [acc]
    return pl.pallas_call(
        functools.partial(project_kernel, head),
        grid_spec=pltpu.PrefetchScalarGridSpec(
            num_scalar_prefetch=1,
            grid=(1,),
            in_specs=[whole, whole] + [half(buffer) for buffer in buffers] + [whole] * len(extra),
            out_specs=out_specs,
            scratch_shapes=[pltpu.VMEM((2 * tokens, 16 * HEAD_DIM), BF16)],
        ),
        out_shape=shapes,
        compiler_params=pltpu.CompilerParams(vmem_limit_bytes=48 << 20),
        cost_estimate=cost(2 * 256 * 2048 * 1536, 9 << 20),
    )(pos, a, b, *buffers, *extra)


def finish_kernel(pos_ref, mine_ref, other_ref, out_ref, stack):
    core = pos_ref[4]
    for yh in range(2):
        for x in range(4):
            stack[pl.ds(pl.multiple_of(core * 192, 64), 192)] = mine_ref[yh, x].astype(F32)
            stack[pl.ds(pl.multiple_of((1 - core) * 192, 64), 192)] = other_ref[yh, x].astype(F32)
            low = (yh * 4 + x) * 384
            out_ref[:, low : low + 384] = stack[...].T.astype(BF16)


def finish(pos, mine, other):
    tokens = mine.shape[3]
    whole = pl.BlockSpec(mine.shape, lambda i, p: (0, 0, 0, 0))
    return pl.pallas_call(
        finish_kernel,
        grid_spec=pltpu.PrefetchScalarGridSpec(
            num_scalar_prefetch=1,
            grid=(1,),
            in_specs=[whole, whole],
            out_specs=pl.BlockSpec((tokens, 3072), lambda i, p: (0, 0)),
            scratch_shapes=[pltpu.VMEM((384, tokens), F32)],
        ),
        out_shape=jax.ShapeDtypeStruct((tokens, 3072), BF16),
        cost_estimate=cost(0, 2 << 20),
        name="finish",
    )(pos, mine, other)


def shift(value, axis, size, step):
    return lax.ppermute(value, axis, [(i, (i + step) % size) for i in range(size)])


def pair_swap(value):
    return lax.ppermute(value, "yl", [(0, 1), (1, 0)])


def cross_swap(value):
    return lax.ppermute(value, ("yh", "yl"), [(1, 2), (2, 1), (3, 0), (0, 3)])


def core_swap(value):
    return lax.ppermute(value, "core", [(0, 1), (1, 0)])


def split_kernel(*refs):
    *blocks, a_ref, b_ref = refs
    for i, block in enumerate(blocks):
        a_ref[i] = block[:ROWS_A]
        b_ref[i] = block[ROWS_A:]


def split_rows(blocks):
    depth = blocks[0].shape[1]
    return pl.pallas_call(
        split_kernel,
        out_shape=[
            jax.ShapeDtypeStruct((len(blocks), rows, depth), BF16) for rows in (ROWS_A, ROWS_B)
        ],
        cost_estimate=cost(0, 1 << 20),
    )(*blocks)


def spread(blocks):
    a, b = split_rows(blocks)
    ax = [a, shift(a, "x", 4, 1), shift(a, "x", 4, -1), shift(a, "x", 4, 2)]
    b_pair, b_cross = pair_swap(b), cross_swap(b)
    by = [b, b_pair, b_cross, cross_swap(b_pair)]
    a, b = jnp.stack(ax), jnp.stack(by)
    a_pair, a_cross = pair_swap(a), cross_swap(a)
    b_up, b_down = shift(b, "x", 4, 1), shift(b, "x", 4, -1)
    a_far = cross_swap(a_pair)
    b_far = (shift(b_up[:2], "x", 4, 1), shift(b_down[2:], "x", 4, -1))
    return (a, a_pair, a_cross, a_far, b, b_up, b_down, *b_far)


def all_to_all(value):
    return lax.all_to_all(value, SEQ, 0, 0, tiled=True)


def per_device(queries, key_rows, value_rows, w_out):
    q, k, v = queries[0], key_rows[0], value_rows[0]
    pos = jnp.stack([lax.axis_index(n) for n in ("yh", "yl", "z", "x", "core")]).astype(jnp.int32)
    wt = w_out.T

    near = {step: shift(wt, "z", 8, -step) for step in NEAR[1:]}
    sent0 = all_to_all(pack(q, k, v, 0))
    far = {
        -3: shift(near[-2], "z", 8, 1),
        3: shift(near[2], "z", 8, -1),
        -4: shift(near[-2], "z", 8, 2),
    }
    weights0 = spread([wt] + [near[step] for step in NEAR[1:]])
    weights1 = spread([far[step] for step in FAR])

    sent1 = all_to_all(pack(q, k, v, 1))
    mixed0 = attend(sent0)
    back0 = all_to_all(mixed0)
    mixed1 = attend(sent1)
    back1 = all_to_all(mixed1)
    groups = (weights0, weights1)
    other0 = core_swap(back0)
    acc = project(pos, back0, other0, groups, 0)
    mine, theirs = project(pos, back1, core_swap(back1), groups, 1, acc)
    return finish(pos, mine, core_swap(theirs))[None]


def solution(mesh):
    fine = Mesh(mesh.devices.reshape(2, 4, 2, 2, 8), DP + SEQ)
    rows = P(DP, SEQ, None)
    return jax.shard_map(
        per_device,
        mesh=fine,
        in_specs=(rows, rows, rows, P(SEQ, DP)),
        out_specs=rows,
        check_vma=False,
    )
```

profile of v0, /device:TPU:1, one launch (start us, length us, event | category | flops | bytes accessed | tf_op | source)
XLA Modules:
  0.0 255.6 jit_solution(6876753773344999514)
XLA Ops:
  0.0 3.9 %shard_map.50 = bf16[16,3,128,128]{3,2,1,0:T(8,128)(2,1)} custom-call(bf16[128,4096]{1,0:T(8,128)(2,1)} %bitcast.26, bf16[128,4096]{1,0:T(8,128)(2,1)} %bitcast.28, bf16[128,4096]{1,0:T(8,128)(2,1)} %bitcast.30), custom_call_target="tpu_custom_call" | custom-call | bytes 5242880 | tf_op jit(solution)/shard_map/pallas_call | solution.py:34
  3.9 10.1 %all-to-all-start.2 = ((bf16[16,3,128,128]{3,2,1,0:T(8,128)(2,1)}), bf16[16,3,128,128]{3,2,1,0:T(8,128)(2,1)S(1)}, u32[]{:S(2)}, u32[]{:S(2)}) async-start(bf16[16,3,128,128]{3,2,1,0:T(8,128)(2,1)} %shard_map.50), calls=%async_computation.2 | async-start | bytes 3145728 | tf_op jit(solution)/shard_map/all_to_all | solution.py:246
  14.0 3.9 %shard_map.46 = bf16[16,3,128,128]{3,2,1,0:T(8,128)(2,1)} custom-call(bf16[128,4096]{1,0:T(8,128)(2,1)} %bitcast.27, bf16[128,4096]{1,0:T(8,128)(2,1)} %bitcast.29, bf16[128,4096]{1,0:T(8,128)(2,1)} %bitcast.31), custom_call_target="tpu_custom_call" | custom-call | bytes 5242880 | tf_op jit(solution)/shard_map/pallas_call | solution.py:34
  18.0 32.4 %all-to-all-done.2.q_ref.k_ref.v_ref = bf16[16,3,128,128]{3,2,1,0:T(8,128)(2,1)S(1)} async-done(((bf16[16,3,128,128]{3,2,1,0:T(8,128)(2,1)}), bf16[16,3,128,128]{3,2,1,0:T(8,128)(2,1)S(1)}, u32[]{:S(2)}, u32[]{:S(2)}) %all-to-all-start.2) | async-done | bytes 1572896 | tf_op jit(solution)/shard_map/all_to_all | solution.py:246
  50.4 6.6 %all-to-all-start = ((bf16[16,3,128,128]{3,2,1,0:T(8,128)(2,1)}), bf16[16,3,128,128]{3,2,1,0:T(8,128)(2,1)S(1)}, u32[]{:S(2)}, u32[]{:S(2)}) async-start(bf16[16,3,128,128]{3,2,1,0:T(8,128)(2,1)} %shard_map.46), calls=%async_computation | async-start | bytes 3145728 | tf_op jit(solution)/shard_map/all_to_all | solution.py:246
  62.2 33.8 %collective-permute-done.3.refs_3_ = bf16[192,256]{1,0:T(8,128)(2,1)S(1)} collective-permute-done((bf16[192,256]{1,0:T(8,128)(2,1)S(1)}, bf16[192,256]{1,0:T(8,128)(2,1)S(1)}, u32[]{:S(2)}, u32[]{:S(2)}) %collective-permute-start.3) | collective-permute-done | bytes 98336 | tf_op jit(solution)/shard_map/ppermute | solution.py:199
  95.9 2.6 %collective-permute-start.18 = (bf16[192,256]{1,0:T(8,128)(2,1)S(1)}, bf16[192,256]{1,0:T(8,128)(2,1)S(1)}, u32[]{:S(2)}, u32[]{:S(2)}) collective-permute-start(bf16[192,256]{1,0:T(8,128)(2,1)S(1)} %collective-permute-done.3.refs_3_), channel_id=1, source_target_pairs={{0,1},{1,2},{2,3},{3,4},{4,5},{5,6},{6,7},{7,0},{8,9},{9,10},{10,1... | collective-permute-start | bytes 294920 | tf_op jit(solution)/shard_map/ppermute | solution.py:199
  103.0 2.7 %collective-permute-start.7 = (bf16[5,80,256]{2,1,0:T(8,128)(2,1)}, bf16[5,80,256]{2,1,0:T(8,128)(2,1)}, u32[]{:S(2)}, u32[]{:S(2)}) collective-permute-start(bf16[5,80,256]{2,1,0:T(8,128)(2,1)} %get-tuple-element.11), channel_id=1, source_target_pairs={{0,64},{32,96},{64,0},{96,32},{1,65},{33,97},{65,1},{97,33},{2,66}... | collective-permute-start | bytes 614408 | tf_op jit(solution)/shard_map/ppermute | solution.py:199
  112.4 4.8 %collective-permute-done.20.refs_2_ = bf16[192,256]{1,0:T(8,128)(2,1)} collective-permute-done((bf16[192,256]{1,0:T(8,128)(2,1)}, bf16[192,256]{1,0:T(8,128)(2,1)}, u32[]{:S(2)}, u32[]{:S(2)}) %collective-permute-start.20) | collective-permute-done | bytes 98336 | tf_op jit(solution)/shard_map/ppermute | solution.py:199
  117.3 2.6 %collective-permute-start.12 = (bf16[5,112,256]{2,1,0:T(8,128)(2,1)}, bf16[5,112,256]{2,1,0:T(8,128)(2,1)}, u32[]{:S(2)}, u32[]{:S(2)}) collective-permute-start(bf16[5,112,256]{2,1,0:T(8,128)(2,1)} %get-tuple-element.12), channel_id=1, source_target_pairs={{8,128},{128,8},{136,0},{0,136},{9,129},{129,9},{137,1},{1,137},{1... | collective-permute-start | bytes 860168 | tf_op jit(solution)/shard_map/ppermute | solution.py:207
  127.8 7.5 %shard_map.51 = bf16[16,128,128]{2,1,0:T(8,128)(2,1)S(1)} custom-call(bf16[16,3,128,128]{3,2,1,0:T(8,128)(2,1)S(1)} %all-to-all-done.2.q_ref.k_ref.v_ref, bf16[16,3,128,128]{3,2,1,0:T(8,128)(2,1)S(1)} %all-to-all-done.2.q_ref.k_ref.v_ref, bf16[16,3,128,128]{3,2,1,0:T(8,128)(2,1)S(1)} %all-to-all-done.2.q_ref.k_ref.v_ref), custom_call_target="tpu_custom_call" | custom-call | flops 2147483648 | bytes 2097152 | tf_op jit(solution)/shard_map/pallas_call | solution.py:64
  138.1 6.8 %all-to-all-start.3 = ((bf16[16,128,128]{2,1,0:T(8,128)(2,1)}), bf16[16,128,128]{2,1,0:T(8,128)(2,1)S(1)}, u32[]{:S(2)}, u32[]{:S(2)}) async-start(bf16[16,128,128]{2,1,0:T(8,128)(2,1)} %copy-done.15), calls=%async_computation.3 | async-start | bytes 1048576 | tf_op jit(solution)/shard_map/all_to_all | solution.py:246
  155.2 5.3 %collective-permute-done.29 = bf16[3,112,256]{2,1,0:T(8,128)(2,1)S(1)} collective-permute-done((bf16[3,112,256]{2,1,0:T(8,128)(2,1)}, bf16[3,112,256]{2,1,0:T(8,128)(2,1)S(1)}, u32[]{:S(2)}, u32[]{:S(2)}) %collective-permute-start.29) | collective-permute-done | bytes 172064 | tf_op jit(solution)/shard_map/ppermute | solution.py:207
  168.5 7.5 %shard_map.47 = bf16[16,128,128]{2,1,0:T(8,128)(2,1)S(1)} custom-call(bf16[16,3,128,128]{3,2,1,0:T(8,128)(2,1)S(1)} %copy-done.9, bf16[16,3,128,128]{3,2,1,0:T(8,128)(2,1)S(1)} %copy-done.9, bf16[16,3,128,128]{3,2,1,0:T(8,128)(2,1)S(1)} %copy-done.9), custom_call_target="tpu_custom_call" | custom-call | flops 2147483648 | bytes 2097152 | tf_op jit(solution)/shard_map/pallas_call | solution.py:64
  176.9 7.0 %all-to-all-start.1 = ((bf16[16,128,128]{2,1,0:T(8,128)(2,1)}), bf16[16,128,128]{2,1,0:T(8,128)(2,1)S(1)}, u32[]{:S(2)}, u32[]{:S(2)}) async-start(bf16[16,128,128]{2,1,0:T(8,128)(2,1)} %copy-done.16), calls=%async_computation.1 | async-start | bytes 1048576 | tf_op jit(solution)/shard_map/all_to_all | solution.py:246
  183.9 2.7 %collective-permute-done.30.refs_14_ = bf16[4,3,112,256]{3,2,1,0:T(8,128)(2,1)} collective-permute-done((bf16[4,3,112,256]{3,2,1,0:T(8,128)(2,1)S(1)}, bf16[4,3,112,256]{3,2,1,0:T(8,128)(2,1)}, u32[]{:S(2)}, u32[]{:S(2)}) %collective-permute-start.30) | collective-permute-done | bytes 688160 | tf_op jit(solution)/shard_map/ppermute | solution.py:199
  188.9 3.3 %collective-permute-start.10 = (bf16[4,5,80,256]{3,2,1,0:T(8,128)(2,1)}, bf16[4,5,80,256]{3,2,1,0:T(8,128)(2,1)}, u32[]{:S(2)}, u32[]{:S(2)}) collective-permute-start(bf16[4,5,80,256]{3,2,1,0:T(8,128)(2,1)} %collective-permute-done.8.refs_1_), channel_id=1, source_target_pairs={{8,128},{128,8},{136,0},{0,136},{9,129},{129,9},{137,1},{1,137},{1... | collective-permute-start | bytes 2457608 | tf_op jit(solution)/shard_map/ppermute | solution.py:207
  193.2 3.6 %collective-permute-start.33 = (bf16[2,3,112,256]{3,2,1,0:T(8,128)(2,1)S(1)}, bf16[2,3,112,256]{3,2,1,0:T(8,128)(2,1)S(1)}, u32[]{:S(2)}, u32[]{:S(2)}) collective-permute-start(bf16[2,3,112,256]{3,2,1,0:T(8,128)(2,1)S(1)} %slice.19), channel_id=1, source_target_pairs={{0,96},{32,0},{64,32},{96,64},{1,97},{33,1},{65,33},{97,65},{2,98}... | collective-permute-start | bytes 1032200 | tf_op jit(solution)/shard_map/ppermute | solution.py:199
  201.5 2.7 %collective-permute-start.17 = (bf16[2,5,112,256]{3,2,1,0:T(8,128)(2,1)}, bf16[2,5,112,256]{3,2,1,0:T(8,128)(2,1)S(1)}, u32[]{:S(2)}, u32[]{:S(2)}) collective-permute-start(bf16[2,5,112,256]{3,2,1,0:T(8,128)(2,1)} %slice.17), channel_id=1, source_target_pairs={{0,96},{32,0},{64,32},{96,64},{1,97},{33,1},{65,33},{97,65},{2,98}... | collective-permute-start | bytes 1720328 | tf_op jit(solution)/shard_map/ppermute | solution.py:199
  204.9 21.3 %collective-permute-start.34 = (bf16[16,128,128]{2,1,0:T(8,128)(2,1)S(1)}, bf16[16,128,128]{2,1,0:T(8,128)(2,1)}, u32[]{:S(2)}, u32[]{:S(2)}) collective-permute-start(bf16[16,128,128]{2,1,0:T(8,128)(2,1)S(1)} %all-to-all-done.3.a_ref), channel_id=1, source_target_pairs={{0,16},{16,0},{1,17},{17,1},{2,18},{18,2},{3,19},{19,3},{4,20},{20... | collective-permute-start | bytes 1572872 | tf_op jit(solution)/shard_map/ppermute | solution.py:211
  233.0 6.0 %shard_map.52.refs_18_ = f32[2,4,192,256]{3,2,1,0:T(8,128)} custom-call(s32[5]{0:T(128)S(1)} %stack.83.pos_ref, bf16[16,128,128]{2,1,0:T(8,128)(2,1)S(1)} %all-to-all-done.3.a_ref, bf16[16,128,128]{2,1,0:T(8,128)(2,1)} %collective-permute-done.34.b_ref, bf16[4,5,80,256]{3,2,1,0:T(8,128)(2,1)} %pad_maximum_fusion.1.refs_0_, ...), custom_call_target="tpu_custom_call" | custom-call | flops 1610612736 | bytes 9437184 | tf_op jit(solution)/shard_map/pallas_call | solution.py:155
  239.1 5.5 %shard_map.53 = (bf16[2,4,192,128]{3,2,1,0:T(8,128)(2,1)S(1)}, bf16[2,4,192,128]{3,2,1,0:T(8,128)(2,1)S(1)}) custom-call(s32[5]{0:T(128)S(1)} %stack.83.pos_ref, bf16[16,128,128]{2,1,0:T(8,128)(2,1)S(1)} %all-to-all-done.1.a_ref, bf16[16,128,128]{2,1,0:T(8,128)(2,1)} %collective-permute-done.b_ref, bf16[4,5,80,256]{3,2,1,0:T(8,128)(2,1)} %pad_maximum_fusion.1.refs_0_, ...), custom_call_target="tpu_custom_call" | custom-call | flops 1610612736 | bytes 9437184 | tf_op jit(solution)/shard_map/pallas_call | solution.py:155
  245.3 5.1 %collective-permute-start.35 = (bf16[2,4,192,128]{3,2,1,0:T(8,128)(2,1)S(1)}, bf16[2,4,192,128]{3,2,1,0:T(8,128)(2,1)S(1)}, u32[]{:S(2)}, u32[]{:S(2)}) collective-permute-start(bf16[2,4,192,128]{3,2,1,0:T(8,128)(2,1)S(1)} %get-tuple-element.16), channel_id=1, source_target_pairs={{0,16},{16,0},{1,17},{17,1},{2,18},{18,2},{3,19},{19,3},{4,20},{20... | collective-permute-start | bytes 1179656 | tf_op jit(solution)/shard_map/ppermute | solution.py:211
  252.6 3.0 %finish.1 = bf16[128,3072]{1,0:T(8,128)(2,1)} custom-call(s32[5]{0:T(128)} %copy-done.18, bf16[2,4,192,128]{3,2,1,0:T(8,128)(2,1)} %copy-done.17, bf16[2,4,192,128]{3,2,1,0:T(8,128)(2,1)} %copy-done.19), custom_call_target="tpu_custom_call" | custom-call | bytes 2097152 | tf_op jit(solution)/shard_map/finish/pallas_call | solution.py:183
  (136 shorter events, 64.4 us)
Async XLA Ops:
  3.9 46.5 %all-to-all-start.2 = ((bf16[16,3,128,128]{3,2,1,0:T(8,128)(2,1)}), bf16[16,3,128,128]{3,2,1,0:T(8,128)(2,1)S(1)}, u32[]{:S(2)}, u32[]{:S(2)}) async-start(bf16[16,3,128,128]{3,2,1,0:T(8,128)(2,1)} %shard_map.50), calls=%async_computation.2 | async-start | bytes 3145728 | tf_op jit(solution)/shard_map/all_to_all | solution.py:246
  50.4 86.5 %all-to-all-start = ((bf16[16,3,128,128]{3,2,1,0:T(8,128)(2,1)}), bf16[16,3,128,128]{3,2,1,0:T(8,128)(2,1)S(1)}, u32[]{:S(2)}, u32[]{:S(2)}) async-start(bf16[16,3,128,128]{3,2,1,0:T(8,128)(2,1)} %shard_map.46), calls=%async_computation | async-start | bytes 3145728 | tf_op jit(solution)/shard_map/all_to_all | solution.py:246
  57.0 38.9 %collective-permute-start.3 = (bf16[192,256]{1,0:T(8,128)(2,1)S(1)}, bf16[192,256]{1,0:T(8,128)(2,1)S(1)}, u32[]{:S(2)}, u32[]{:S(2)}) collective-permute-start(bf16[192,256]{1,0:T(8,128)(2,1)S(1)} %bitcast.42), channel_id=1, source_target_pairs={{0,2},{1,3},{2,4},{3,5},{4,6},{5,7},{6,0},{7,1},{8,10},{9,11},{10,... | collective-permute-start | bytes 294920 | tf_op jit(solution)/shard_map/ppermute | solution.py:199
  59.4 40.5 %collective-permute-start.1 = (bf16[192,256]{1,0:T(8,128)(2,1)S(1)}, bf16[192,256]{1,0:T(8,128)(2,1)S(1)}, u32[]{:S(2)}, u32[]{:S(2)}) collective-permute-start(bf16[192,256]{1,0:T(8,128)(2,1)S(1)} %bitcast.43), channel_id=1, source_target_pairs={{0,1},{1,2},{2,3},{3,4},{4,5},{5,6},{6,7},{7,0},{8,9},{9,10},{10,1... | collective-permute-start | bytes 294920 | tf_op jit(solution)/shard_map/ppermute | solution.py:199
  60.6 39.3 %collective-permute-start.2 = (bf16[192,256]{1,0:T(8,128)(2,1)S(1)}, bf16[192,256]{1,0:T(8,128)(2,1)S(1)}, u32[]{:S(2)}, u32[]{:S(2)}) collective-permute-start(bf16[192,256]{1,0:T(8,128)(2,1)S(1)} %bitcast.44), channel_id=1, source_target_pairs={{0,7},{1,0},{2,1},{3,2},{4,3},{5,4},{6,5},{7,6},{8,15},{9,8},{10,9... | collective-permute-start | bytes 294920 | tf_op jit(solution)/shard_map/ppermute | solution.py:199
  62.1 39.1 %collective-permute-start.4 = (bf16[192,256]{1,0:T(8,128)(2,1)S(1)}, bf16[192,256]{1,0:T(8,128)(2,1)}, u32[]{:S(2)}, u32[]{:S(2)}) collective-permute-start(bf16[192,256]{1,0:T(8,128)(2,1)S(1)} %bitcast.45), channel_id=1, source_target_pairs={{0,6},{1,7},{2,0},{3,1},{4,2},{5,3},{6,4},{7,5},{8,14},{9,15},{10,... | collective-permute-start | bytes 294920 | tf_op jit(solution)/shard_map/ppermute | solution.py:199
  103.0 18.6 %collective-permute-start.7 = (bf16[5,80,256]{2,1,0:T(8,128)(2,1)}, bf16[5,80,256]{2,1,0:T(8,128)(2,1)}, u32[]{:S(2)}, u32[]{:S(2)}) collective-permute-start(bf16[5,80,256]{2,1,0:T(8,128)(2,1)} %get-tuple-element.11), channel_id=1, source_target_pairs={{0,64},{32,96},{64,0},{96,32},{1,65},{33,97},{65,1},{97,33},{2,66}... | collective-permute-start | bytes 614408 | tf_op jit(solution)/shard_map/ppermute | solution.py:199
  108.6 18.5 %collective-permute-start.11 = (bf16[5,112,256]{2,1,0:T(8,128)(2,1)}, bf16[5,112,256]{2,1,0:T(8,128)(2,1)S(1)}, u32[]{:S(2)}, u32[]{:S(2)}) collective-permute-start(bf16[5,112,256]{2,1,0:T(8,128)(2,1)} %get-tuple-element.12), channel_id=1, source_target_pairs={{0,8},{8,0},{1,9},{9,1},{2,10},{10,2},{3,11},{11,3},{4,12},{12,4},... | collective-permute-start | bytes 860168 | tf_op jit(solution)/shard_map/ppermute | solution.py:203
  117.3 31.8 %collective-permute-start.12 = (bf16[5,112,256]{2,1,0:T(8,128)(2,1)}, bf16[5,112,256]{2,1,0:T(8,128)(2,1)}, u32[]{:S(2)}, u32[]{:S(2)}) collective-permute-start(bf16[5,112,256]{2,1,0:T(8,128)(2,1)} %get-tuple-element.12), channel_id=1, source_target_pairs={{8,128},{128,8},{136,0},{0,136},{9,129},{129,9},{137,1},{1,137},{1... | collective-permute-start | bytes 860168 | tf_op jit(solution)/shard_map/ppermute | solution.py:207
  124.2 20.7 %collective-permute-start.21 = (bf16[3,80,256]{2,1,0:T(8,128)(2,1)}, bf16[3,80,256]{2,1,0:T(8,128)(2,1)}, u32[]{:S(2)}, u32[]{:S(2)}) collective-permute-start(bf16[3,80,256]{2,1,0:T(8,128)(2,1)} %get-tuple-element.13), channel_id=1, source_target_pairs={{0,32},{32,64},{64,96},{96,0},{1,33},{33,65},{65,97},{97,1},{2,34}... | collective-permute-start | bytes 368648 | tf_op jit(solution)/shard_map/ppermute | solution.py:199
  127.1 38.9 %collective-permute-start.8 = (bf16[4,5,80,256]{3,2,1,0:T(8,128)(2,1)}, bf16[4,5,80,256]{3,2,1,0:T(8,128)(2,1)}, u32[]{:S(2)}, u32[]{:S(2)}) collective-permute-start(bf16[4,5,80,256]{3,2,1,0:T(8,128)(2,1)} %pad_maximum_fusion.1.refs_0_), channel_id=1, source_target_pairs={{0,8},{8,0},{1,9},{9,1},{2,10},{10,2},{3,11},{11,3},{4,12},{12,4},... | collective-permute-start | bytes 2457608 | tf_op jit(solution)/shard_map/ppermute | solution.py:203
  127.7 22.5 %collective-permute-start.13 = (bf16[5,112,256]{2,1,0:T(8,128)(2,1)S(1)}, bf16[5,112,256]{2,1,0:T(8,128)(2,1)}, u32[]{:S(2)}, u32[]{:S(2)}) collective-permute-start(bf16[5,112,256]{2,1,0:T(8,128)(2,1)S(1)} %collective-permute-done.11), channel_id=1, source_target_pairs={{8,128},{128,8},{136,0},{0,136},{9,129},{129,9},{137,1},{1,137},{1... | collective-permute-start | bytes 860168 | tf_op jit(solution)/shard_map/ppermute | solution.py:207
  138.1 38.7 %all-to-all-start.3 = ((bf16[16,128,128]{2,1,0:T(8,128)(2,1)}), bf16[16,128,128]{2,1,0:T(8,128)(2,1)S(1)}, u32[]{:S(2)}, u32[]{:S(2)}) async-start(bf16[16,128,128]{2,1,0:T(8,128)(2,1)} %copy-done.15), calls=%async_computation.3 | async-start | bytes 1048576 | tf_op jit(solution)/shard_map/all_to_all | solution.py:246
  154.1 34.8 %collective-permute-start.14 = (bf16[4,5,112,256]{3,2,1,0:T(8,128)(2,1)}, bf16[4,5,112,256]{3,2,1,0:T(8,128)(2,1)}, u32[]{:S(2)}, u32[]{:S(2)}) collective-permute-start(bf16[4,5,112,256]{3,2,1,0:T(8,128)(2,1)} %pad_maximum_fusion.refs_4_), channel_id=1, source_target_pairs={{0,32},{32,64},{64,96},{96,0},{1,33},{33,65},{65,97},{97,1},{2,34}... | collective-permute-start | bytes 3440648 | tf_op jit(solution)/shard_map/ppermute | solution.py:199
  160.6 32.6 %collective-permute-start.15 = (bf16[4,5,112,256]{3,2,1,0:T(8,128)(2,1)}, bf16[4,5,112,256]{3,2,1,0:T(8,128)(2,1)}, u32[]{:S(2)}, u32[]{:S(2)}) collective-permute-start(bf16[4,5,112,256]{3,2,1,0:T(8,128)(2,1)} %pad_maximum_fusion.refs_4_), channel_id=1, source_target_pairs={{0,96},{32,0},{64,32},{96,64},{1,97},{33,1},{65,33},{97,65},{2,98}... | collective-permute-start | bytes 3440648 | tf_op jit(solution)/shard_map/ppermute | solution.py:199
  164.3 22.3 %collective-permute-start.30 = (bf16[4,3,112,256]{3,2,1,0:T(8,128)(2,1)S(1)}, bf16[4,3,112,256]{3,2,1,0:T(8,128)(2,1)}, u32[]{:S(2)}, u32[]{:S(2)}) collective-permute-start(bf16[4,3,112,256]{3,2,1,0:T(8,128)(2,1)S(1)} %pad_maximum_fusion.2.refs_13_), channel_id=1, source_target_pairs={{0,32},{32,64},{64,96},{96,0},{1,33},{33,65},{65,97},{97,1},{2,34}... | collective-permute-start | bytes 2064392 | tf_op jit(solution)/shard_map/ppermute | solution.py:199
  165.5 35.2 %collective-permute-start.9 = (bf16[4,5,80,256]{3,2,1,0:T(8,128)(2,1)}, bf16[4,5,80,256]{3,2,1,0:T(8,128)(2,1)}, u32[]{:S(2)}, u32[]{:S(2)}) collective-permute-start(bf16[4,5,80,256]{3,2,1,0:T(8,128)(2,1)} %pad_maximum_fusion.1.refs_0_), channel_id=1, source_target_pairs={{8,128},{128,8},{136,0},{0,136},{9,129},{129,9},{137,1},{1,137},{1... | collective-permute-start | bytes 2457608 | tf_op jit(solution)/shard_map/ppermute | solution.py:207
  166.0 22.9 %collective-permute-start.31 = (bf16[4,3,112,256]{3,2,1,0:T(8,128)(2,1)S(1)}, bf16[4,3,112,256]{3,2,1,0:T(8,128)(2,1)}, u32[]{:S(2)}, u32[]{:S(2)}) collective-permute-start(bf16[4,3,112,256]{3,2,1,0:T(8,128)(2,1)S(1)} %pad_maximum_fusion.2.refs_13_), channel_id=1, source_target_pairs={{0,96},{32,0},{64,32},{96,64},{1,97},{33,1},{65,33},{97,65},{2,98}... | collective-permute-start | bytes 2064392 | tf_op jit(solution)/shard_map/ppermute | solution.py:199
  176.9 50.2 %all-to-all-start.1 = ((bf16[16,128,128]{2,1,0:T(8,128)(2,1)}), bf16[16,128,128]{2,1,0:T(8,128)(2,1)S(1)}, u32[]{:S(2)}, u32[]{:S(2)}) async-start(bf16[16,128,128]{2,1,0:T(8,128)(2,1)} %copy-done.16), calls=%async_computation.1 | async-start | bytes 1048576 | tf_op jit(solution)/shard_map/all_to_all | solution.py:246
  188.9 38.2 %collective-permute-start.10 = (bf16[4,5,80,256]{3,2,1,0:T(8,128)(2,1)}, bf16[4,5,80,256]{3,2,1,0:T(8,128)(2,1)}, u32[]{:S(2)}, u32[]{:S(2)}) collective-permute-start(bf16[4,5,80,256]{3,2,1,0:T(8,128)(2,1)} %collective-permute-done.8.refs_1_), channel_id=1, source_target_pairs={{8,128},{128,8},{136,0},{0,136},{9,129},{129,9},{137,1},{1,137},{1... | collective-permute-start | bytes 2457608 | tf_op jit(solution)/shard_map/ppermute | solution.py:207
  193.2 33.1 %collective-permute-start.33 = (bf16[2,3,112,256]{3,2,1,0:T(8,128)(2,1)S(1)}, bf16[2,3,112,256]{3,2,1,0:T(8,128)(2,1)S(1)}, u32[]{:S(2)}, u32[]{:S(2)}) collective-permute-start(bf16[2,3,112,256]{3,2,1,0:T(8,128)(2,1)S(1)} %slice.19), channel_id=1, source_target_pairs={{0,96},{32,0},{64,32},{96,64},{1,97},{33,1},{65,33},{97,65},{2,98}... | collective-permute-start | bytes 1032200 | tf_op jit(solution)/shard_map/ppermute | solution.py:199
  200.7 26.4 %collective-permute-start.16 = (bf16[2,5,112,256]{3,2,1,0:T(8,128)(2,1)}, bf16[2,5,112,256]{3,2,1,0:T(8,128)(2,1)S(1)}, u32[]{:S(2)}, u32[]{:S(2)}) collective-permute-start(bf16[2,5,112,256]{3,2,1,0:T(8,128)(2,1)} %slice.16), channel_id=1, source_target_pairs={{0,32},{32,64},{64,96},{96,0},{1,33},{33,65},{65,97},{97,1},{2,34}... | collective-permute-start | bytes 1720328 | tf_op jit(solution)/shard_map/ppermute | solution.py:199
  201.5 25.6 %collective-permute-start.17 = (bf16[2,5,112,256]{3,2,1,0:T(8,128)(2,1)}, bf16[2,5,112,256]{3,2,1,0:T(8,128)(2,1)S(1)}, u32[]{:S(2)}, u32[]{:S(2)}) collective-permute-start(bf16[2,5,112,256]{3,2,1,0:T(8,128)(2,1)} %slice.17), channel_id=1, source_target_pairs={{0,96},{32,0},{64,32},{96,64},{1,97},{33,1},{65,33},{97,65},{2,98}... | collective-permute-start | bytes 1720328 | tf_op jit(solution)/shard_map/ppermute | solution.py:199
  204.9 23.0 %collective-permute-start.34 = (bf16[16,128,128]{2,1,0:T(8,128)(2,1)S(1)}, bf16[16,128,128]{2,1,0:T(8,128)(2,1)}, u32[]{:S(2)}, u32[]{:S(2)}) collective-permute-start(bf16[16,128,128]{2,1,0:T(8,128)(2,1)S(1)} %all-to-all-done.3.a_ref), channel_id=1, source_target_pairs={{0,16},{16,0},{1,17},{17,1},{2,18},{18,2},{3,19},{19,3},{4,20},{20... | collective-permute-start | bytes 1572872 | tf_op jit(solution)/shard_map/ppermute | solution.py:211
  (47 other events, 441.3 us)
where the time goes:
time: 257 us; the launch traced here: 256 us
  starting transfers between devices  102 us (40%)
  waiting for transfers between devices  86 us (33%)
  Pallas kernels  41 us (16%)
  local copies, waits for them, and re-layouts  19.6 us (8%)
  other arithmetic  6.63 us (3%)
    ppermute x21, waiting for transfers between devices, shift(): lax.ppermute(value, axis, [(i, (i + step) % size) for i in range(size)])  45.5 us
    all_to_all x4, waiting for transfers between devices, all_to_all(): return lax.all_to_all(value, SEQ, 0, 0, tiled=True)  32.4 us
    all_to_all x4, starting transfers between devices, all_to_all(): return lax.all_to_all(value, SEQ, 0, 0, tiled=True)  30.6 us
    ppermute x21, starting transfers between devices, shift(): lax.ppermute(value, axis, [(i, (i + step) % size) for i in range(size)])  30.4 us
    ppermute x3, starting transfers between devices, core_swap(): return lax.ppermute(value, 'core', [(0, 1), (1, 0)])  26.5 us
    pallas_call x2, Pallas kernels, attend(): pl.pallas_call(functools.partial(attend_kernel, 256), grid=(n // per,), i...  15 us
    unnamed x62, local copies, waits for them, and re-layouts  13.6 us
    pallas_call x2, Pallas kernels, project(): pl.pallas_call(functools.partial(project_kernel, head), grid_spec=pltpu.P...  11.5 us
  transfers between devices with their start and end apart: 40, of which 12 were waited for; matrix products, arithmetic and copies ran while one was open for 5% of the time, Pallas kernels for 11%

commit v1 on v0

v1 whole, which is shorter than its diff:
```python
import functools

import jax
import jax.numpy as jnp
import numpy as np
from jax import lax
from jax.experimental import pallas as pl
from jax.experimental.pallas import tpu as pltpu
from jax.sharding import Mesh
from jax.sharding import PartitionSpec as P

HEAD_DIM = 128
SCALE = float(np.log2(np.e) / np.sqrt(HEAD_DIM))
DP = ("yh", "x", "core")
SEQ = ("yl", "z")
BF16 = jnp.bfloat16
F32 = jnp.float32


def cost(flops, nbytes, exps=0):
    return pl.CostEstimate(flops=flops, bytes_accessed=nbytes, transcendentals=exps)


def pack_kernel(head, q_ref, k_ref, v_ref, out_ref, sem):
    copies = [
        pltpu.make_async_copy(
            ref.at[:, pl.ds(group * 256 + head * HEAD_DIM, HEAD_DIM)],
            out_ref.at[group, index],
            sem.at[group, index],
        )
        for group in range(16)
        for index, ref in enumerate((q_ref, k_ref, v_ref))
    ]
    for copy in copies:
        copy.start()
    for copy in copies:
        copy.wait()


def pack(queries, key_rows, value_rows, head):
    tokens = queries.shape[0]
    return pl.pallas_call(
        functools.partial(pack_kernel, head),
        in_specs=[pl.BlockSpec(memory_space=pltpu.HBM)] * 3,
        out_shape=pltpu.HBM((16, 3, tokens, HEAD_DIM), BF16),
        scratch_shapes=[pltpu.SemaphoreType.DMA((16, 3))],
        compiler_params=pltpu.CompilerParams(vmem_limit_bytes=60 * 1024 * 1024),
        cost_estimate=cost(0, 5 << 20),
    )(queries, key_rows, value_rows)


def attend_rows(rows, keys, values):
    scores = lax.dot_general(
        rows, keys, (((1,), (1,)), ((), ())), preferred_element_type=F32
    )
    largest = jnp.max(scores, axis=1, keepdims=True)
    weights = jnp.exp2((scores - largest) * SCALE)
    total = jnp.sum(weights, axis=1, keepdims=True)
    mixed = jnp.dot(weights.astype(BF16), values, preferred_element_type=F32)
    return (mixed / total).astype(BF16)


def attend_kernel(sub, q_ref, k_ref, v_ref, o_ref):
    keys = k_ref[:, 0].reshape(-1, HEAD_DIM)
    values = v_ref[:, 0].reshape(-1, HEAD_DIM)
    rows = q_ref[:, 0].reshape(-1, HEAD_DIM)
    pieces = [
        attend_rows(rows[low : low + sub], keys, values) for low in range(0, rows.shape[0], sub)
    ]
    o_ref[...] = jnp.concatenate(pieces, 0).reshape(o_ref.shape)


def attend(arrived):
    n, _, tokens, _ = arrived.shape
    per = 4
    return pl.pallas_call(
        functools.partial(attend_kernel, 256),
        grid=(n // per,),
        in_specs=[
            pl.BlockSpec((per, 1, tokens, HEAD_DIM), lambda i: (i, 0, 0, 0)),
            pl.BlockSpec((n, 1, tokens, HEAD_DIM), lambda i: (0, 1, 0, 0)),
            pl.BlockSpec((n, 1, tokens, HEAD_DIM), lambda i: (0, 2, 0, 0)),
        ],
        out_specs=pl.BlockSpec((per, tokens, HEAD_DIM), lambda i: (i, 0, 0)),
        out_shape=pltpu.HBM((n, tokens, HEAD_DIM), BF16),
        compiler_params=pltpu.CompilerParams(vmem_limit_bytes=24 << 20),
        cost_estimate=cost(4 * 2048 * 2048 * 128, 2 << 20, 2048 * 2048),
    )(arrived, arrived, arrived)


NEAR = (0, -1, 1, -2, 2)
FAR = (-3, 3, -4)
Z_OFFSETS = NEAR + FAR
X_OFFSETS = (0, -1, 1, 2)
ROWS_A, ROWS_B = 80, 112


def gather_features(pos_ref, features, a_rel):
    tokens = features.shape[2]
    yl, z = pos_ref[1], pos_ref[2]
    for half in range(2):
        group_y = yl if half == 0 else 1 - yl
        for i, offset in enumerate(Z_OFFSETS):
            group = group_y * 8 + lax.rem(z + (8 + offset), 8)
            low = (half * 8 + i) * HEAD_DIM
            for core in range(2):
                a_rel[core * tokens : (core + 1) * tokens, low : low + HEAD_DIM] = features[
                    core, group
                ]


def weight_rows(buffers, same):
    own, pair, cross, far, *b_parts = buffers
    columns = []
    for half in range(2):
        part_a = ((own, pair) if same else (far, cross))[half]
        y = ((0, 1) if same else (3, 2))[half]
        for i in range(own.shape[1]):
            rows = [part_a[:, i].reshape(4 * ROWS_A, HEAD_DIM)]
            rows += [b_parts[2 * j + y // 2][y % 2, i] for j in range(4)]
            columns.append(jnp.concatenate(rows, axis=0))
    return jnp.concatenate(columns, axis=1)


def load_kernel(head, *refs):
    count = len(refs[1:-1]) // 2
    sources, targets, sem = refs[1 : 1 + count], refs[1 + count : -1], refs[-1]
    copies = [
        pltpu.make_async_copy(source.at[:, :, head], target, sem.at[i])
        for i, (source, target) in enumerate(zip(sources, targets))
    ]
    for copy in copies:
        copy.start()
    for copy in copies:
        copy.wait()


def load(ready, buffers, head):
    shapes = [(*buffer.shape[:2], *buffer.shape[3:]) for buffer in buffers]
    return pl.pallas_call(
        functools.partial(load_kernel, head),
        in_specs=[pl.BlockSpec(memory_space=pl.ANY)] * (1 + len(buffers)),
        out_specs=[pl.BlockSpec(memory_space=pltpu.VMEM)] * len(buffers),
        out_shape=[jax.ShapeDtypeStruct(shape, BF16) for shape in shapes],
        scratch_shapes=[pltpu.SemaphoreType.DMA((len(buffers),))],
        compiler_params=pltpu.CompilerParams(vmem_limit_bytes=16 << 20),
        cost_estimate=cost(0, 8 << 20),
    )(ready, *buffers)


def project_kernel(head, pos_ref, a_ref, b_ref, *refs):
    buffers, refs = refs[:12], refs[12:]
    if head == 0:
        out_ref, features, a_rel, sem = refs
    else:
        acc_ref, mine_ref, theirs_ref, features, a_rel, sem = refs
    copies = [
        pltpu.make_async_copy(ref, features.at[i], sem.at[i])
        for i, ref in enumerate((a_ref, b_ref))
    ]
    for copy in copies:
        copy.start()
    for copy in copies:
        copy.wait()
    gather_features(pos_ref, features, a_rel)
    tokens = a_ref.shape[1]
    for same in (True, False):
        yh = pos_ref[0] if same else 1 - pos_ref[0]
        total = lax.dot_general(
            weight_rows(buffers, same),
            a_rel[...],
            (((1,), (1,)), ((), ())),
            preferred_element_type=F32,
        )
        for j, offset in enumerate(X_OFFSETS):
            x = lax.rem(pos_ref[3] + (4 + offset), 4)
            first = 4 * ROWS_A + j * ROWS_B
            parts = (
                (0, ROWS_A, total[j * ROWS_A : (j + 1) * ROWS_A]),
                (ROWS_A, 192, total[first : first + ROWS_B]),
            )
            for low, high, part in parts:
                if head == 0:
                    out_ref[yh, x, low:high] = part
                else:
                    part = part + acc_ref[yh, x, low:high]
                    mine_ref[yh, x, low:high] = part[:, :tokens].astype(BF16)
                    theirs_ref[yh, x, low:high] = part[:, tokens:].astype(BF16)


def project(pos, a, b, buffers, head, acc=()):
    tokens = a.shape[1]
    anywhere, vmem = (pl.BlockSpec(memory_space=space) for space in (pl.ANY, pltpu.VMEM))
    if head == 0:
        shapes, out_specs = pltpu.HBM((2, 4, 192, 2 * tokens), F32), vmem
    else:
        shapes = [jax.ShapeDtypeStruct((2, 4, 192, tokens), BF16)] * 2
        out_specs = [vmem, vmem]
    return pl.pallas_call(
        functools.partial(project_kernel, head),
        grid_spec=pltpu.PrefetchScalarGridSpec(
            num_scalar_prefetch=1,
            grid=(1,),
            in_specs=[anywhere] * 2 + [vmem] * (len(buffers) + len(acc)),
            out_specs=out_specs,
            scratch_shapes=[
                pltpu.VMEM((2, *a.shape), BF16),
                pltpu.VMEM((2 * tokens, 16 * HEAD_DIM), BF16),
                pltpu.SemaphoreType.DMA((2,)),
            ],
        ),
        out_shape=shapes,
        compiler_params=pltpu.CompilerParams(vmem_limit_bytes=24 << 20),
        cost_estimate=cost(2 * 256 * 2048 * 1536, 9 << 20),
    )(pos, a, b, *buffers, *acc)


def finish_kernel(pos_ref, mine_ref, other_ref, out_ref, mine, other, stack, sem):
    core = pos_ref[4]
    copies = [
        pltpu.make_async_copy(source, target, sem.at[i])
        for i, (source, target) in enumerate(((mine_ref, mine), (other_ref, other)))
    ]
    for copy in copies:
        copy.start()
    for copy in copies:
        copy.wait()
    for yh in range(2):
        for x in range(4):
            block = stack.at[yh * 4 + x]
            block[pl.ds(pl.multiple_of(core * 192, 64), 192)] = mine[yh, x]
            block[pl.ds(pl.multiple_of((1 - core) * 192, 64), 192)] = other[yh, x]
            low = (yh * 4 + x) * 384
            out_ref[:, low : low + 384] = block[...].T


def finish(pos, mine, other):
    tokens = mine.shape[3]
    anywhere = pl.BlockSpec(memory_space=pl.ANY)
    return pl.pallas_call(
        finish_kernel,
        grid_spec=pltpu.PrefetchScalarGridSpec(
            num_scalar_prefetch=1,
            grid=(1,),
            in_specs=[anywhere, anywhere],
            out_specs=pl.BlockSpec((tokens, 3072), lambda i, p: (0, 0)),
            scratch_shapes=[
                pltpu.VMEM(mine.shape, BF16),
                pltpu.VMEM(mine.shape, BF16),
                pltpu.VMEM((8, 384, tokens), BF16),
                pltpu.SemaphoreType.DMA((2,)),
            ],
        ),
        out_shape=jax.ShapeDtypeStruct((tokens, 3072), BF16),
        compiler_params=pltpu.CompilerParams(vmem_limit_bytes=8 << 20),
        cost_estimate=cost(0, 2 << 20),
        name="finish",
    )(pos, mine, other)


def shift(value, axis, size, step):
    return lax.ppermute(value, axis, [(i, (i + step) % size) for i in range(size)])


def pair_swap(value):
    return lax.ppermute(value, "yl", [(0, 1), (1, 0)])


def cross_swap(value):
    return lax.ppermute(value, ("yh", "yl"), [(1, 2), (2, 1), (3, 0), (0, 3)])


def core_swap(value):
    return lax.ppermute(value, "core", [(0, 1), (1, 0)])


def split_kernel(*refs):
    *blocks, a_ref, b_ref = refs
    for i, block in enumerate(blocks):
        for head in range(2):
            lanes = slice(head * HEAD_DIM, (head + 1) * HEAD_DIM)
            a_ref[i, head] = block[:ROWS_A, lanes]
            b_ref[i, head] = block[ROWS_A:, lanes]


def split_rows(blocks):
    return pl.pallas_call(
        split_kernel,
        out_shape=[
            jax.ShapeDtypeStruct((len(blocks), 2, rows, HEAD_DIM), BF16) for rows in (ROWS_A, ROWS_B)
        ],
        compiler_params=pltpu.CompilerParams(vmem_limit_bytes=8 << 20),
        cost_estimate=cost(0, 1 << 20),
    )(*blocks)


def spread(blocks):
    a, b = split_rows(blocks)
    b_pair, b_cross = pair_swap(b), cross_swap(b)
    a_up, a_down = shift(a, "x", 4, 1), shift(a, "x", 4, -1)
    b_far, a_up2 = cross_swap(b_pair), shift(a_up, "x", 4, 1)
    near = jnp.stack([b, b_pair])
    a, far = jnp.stack([a, a_up, a_down, a_up2]), jnp.stack([b_cross, b_far])
    up, down = [shift(near, "x", 4, 1)], [shift(near, "x", 4, -1)]
    a_pair, a_cross = pair_swap(a), cross_swap(a)
    up.append(shift(far, "x", 4, 1))
    down.append(shift(far, "x", 4, -1))
    a_far = cross_swap(a_pair)
    last = [shift(up[0], "x", 4, 1), shift(down[1], "x", 4, -1)]
    return (a, a_pair, a_cross, a_far, near, far, *up, *down, *last)


def all_to_all(value):
    return lax.all_to_all(value, SEQ, 0, 0, tiled=True)


def per_device(queries, key_rows, value_rows, w_out):
    q, k, v = queries[0], key_rows[0], value_rows[0]
    pos = jnp.stack([lax.axis_index(n) for n in ("yh", "yl", "z", "x", "core")]).astype(jnp.int32)
    wt = w_out.T

    near = {step: shift(wt, "z", 8, -step) for step in NEAR[1:]}
    packed0 = pack(q, k, v, 0)
    sent0 = all_to_all(packed0)
    far = {
        -3: shift(near[-2], "z", 8, 1),
        3: shift(near[2], "z", 8, -1),
        -4: shift(near[-2], "z", 8, 2),
    }
    weights = spread([wt] + [near[step] for step in NEAR[1:]] + [far[step] for step in FAR])

    packed1 = pack(q, k, v, 1)
    sent1 = all_to_all(packed1)
    mixed0 = attend(sent0)
    back0 = all_to_all(mixed0)
    mixed1 = attend(sent1)
    back1 = all_to_all(mixed1)
    other0 = core_swap(back0)
    rows0 = load(back0, weights, 0)
    acc = project(pos, back0, other0, rows0, 0)
    other1 = core_swap(back1)
    rows1 = load(back1, weights, 1)
    mine, theirs = project(pos, back1, other1, rows1, 1, (acc,))
    return finish(pos, mine, core_swap(theirs))[None]


def solution(mesh):
    fine = Mesh(mesh.devices.reshape(2, 4, 2, 2, 8), DP + SEQ)
    rows = P(DP, SEQ, None)
    return jax.shard_map(
        per_device,
        mesh=fine,
        in_specs=(rows, rows, rows, P(SEQ, DP)),
        out_specs=rows,
        check_vma=False,
    )
```

time: 257 us -> 229 us (0.89)
  local copies, waits for them, and re-layouts: 19.6 us -> 3.43 us
  starting transfers between devices: 102 us -> 89.6 us
  waiting for transfers between devices: 86 us -> 92.9 us
  other arithmetic: 6.63 us -> 2.61 us
    unnamed x62 -> x10, local copies, waits for them, and re-layouts: 13.6 us -> 3.35 us
    ppermute x21 -> x16, waiting for transfers between devices: 45.5 us -> 54.1 us  [shift(): lax.ppermute(value, axis, [(i, (i + step) % size) for i in range(size)])]
    ppermute x21 -> x16, starting transfers between devices: 30.4 us -> 22 us  [shift(): lax.ppermute(value, axis, [(i, (i + step) % size) for i in range(size)])]
    slice x4 -> x0, local copies, waits for them, and re-layouts: 5.88 us -> none  [spread(): b_far = (shift(b_up[:2], 'x', 4, 1), shift(b_down[2:], 'x', 4, -1))]
    another operation x4 -> x3, other arithmetic: 6.63 us -> 2.61 us  [the longest x2 1.41 us: spread(): a, far = (jnp.stack([a, a_up, a_down, a_up2]), jnp.stack([b_cross, b_far]))]
    pallas_call x2 -> x1, Pallas kernels: 3.63 us -> 0.14 us  [split_rows(): pl.pallas_call(split_kernel, out_shape=[jax.ShapeDtypeStruct((len(blocks)...]
    pallas_call x2 -> x4, Pallas kernels: 7.85 us -> 10.9 us  [the longest x2 5.92 us: pack(): pl.pallas_call(functools.partial(pack_kernel, head), in_specs=[pl.BlockSp...]
    ppermute x8 -> x4, starting transfers between devices: 11.2 us -> 8.22 us  [cross_swap(): return lax.ppermute(value, ('yh', 'yl'), [(1, 2), (2, 1), (3, 0), (0, 3)])]
  transfers between devices with their start and end apart: 40 -> 29, of which waited for: 12 -> 10; matrix products, arithmetic and copies ran while one was open for 5% -> 1% of each run, Pallas kernels for 11% -> 13%
where the time goes in v1:
time: 229 us; the launch traced here: 228 us
  waiting for transfers between devices  92.9 us (41%)
  starting transfers between devices  89.6 us (39%)
  Pallas kernels  39.2 us (17%)
  local copies, waits for them, and re-layouts  3.43 us (1%)
  other arithmetic  2.61 us (1%)
    ppermute x16, waiting for transfers between devices, shift(): lax.ppermute(value, axis, [(i, (i + step) % size) for i in range(size)])  54.1 us
    all_to_all x4, waiting for transfers between devices, all_to_all(): return lax.all_to_all(value, SEQ, 0, 0, tiled=True)  33.4 us
    all_to_all x4, starting transfers between devices, all_to_all(): return lax.all_to_all(value, SEQ, 0, 0, tiled=True)  33.2 us
    ppermute x3, starting transfers between devices, core_swap(): return lax.ppermute(value, 'core', [(0, 1), (1, 0)])  25.5 us
    ppermute x16, starting transfers between devices, shift(): lax.ppermute(value, axis, [(i, (i + step) % size) for i in range(size)])  22 us
    pallas_call x2, Pallas kernels, attend(): pl.pallas_call(functools.partial(attend_kernel, 256), grid=(n // per,), i...  17.5 us
    pallas_call x2, Pallas kernels, project(): pl.pallas_call(functools.partial(project_kernel, head), grid_spec=pltpu.P...  8.64 us
    ppermute x4, starting transfers between devices, cross_swap(): return lax.ppermute(value, ('yh', 'yl'), [(1, 2), (2, 1), (3, 0), (0, 3)])  8.22 us
  transfers between devices with their start and end apart: 29, of which 10 were waited for; matrix products, arithmetic and copies ran while one was open for 1% of the time, Pallas kernels for 13%

profile of v1, /device:TPU:1, one launch (start us, length us, event | category | flops | bytes accessed | tf_op | source)
XLA Modules:
  0.0 228.1 jit_solution(8954452222734653002)
XLA Ops:
  0.0 3.0 %shard_map.50 = bf16[16,3,128,128]{3,2,1,0:T(8,128)(2,1)} custom-call(bf16[128,4096]{1,0:T(8,128)(2,1)} %bitcast.25, bf16[128,4096]{1,0:T(8,128)(2,1)} %bitcast.27, bf16[128,4096]{1,0:T(8,128)(2,1)} %bitcast.29), custom_call_target="tpu_custom_call" | custom-call | bytes 5242880 | tf_op jit(solution)/shard_map/pallas_call | solution.py:42
  3.0 10.1 %all-to-all-start.2 = ((bf16[16,3,128,128]{3,2,1,0:T(8,128)(2,1)}), bf16[16,3,128,128]{3,2,1,0:T(8,128)(2,1)S(1)}, u32[]{:S(2)}, u32[]{:S(2)}) async-start(bf16[16,3,128,128]{3,2,1,0:T(8,128)(2,1)} %shard_map.50), calls=%async_computation.2 | async-start | bytes 3145728 | tf_op jit(solution)/shard_map/all_to_all | solution.py:314
  13.1 2.9 %shard_map.46 = bf16[16,3,128,128]{3,2,1,0:T(8,128)(2,1)} custom-call(bf16[128,4096]{1,0:T(8,128)(2,1)} %bitcast.26, bf16[128,4096]{1,0:T(8,128)(2,1)} %bitcast.28, bf16[128,4096]{1,0:T(8,128)(2,1)} %bitcast.30), custom_call_target="tpu_custom_call" | custom-call | bytes 5242880 | tf_op jit(solution)/shard_map/pallas_call | solution.py:42
  16.1 33.4 %all-to-all-done.2.q_ref.k_ref.v_ref = bf16[16,3,128,128]{3,2,1,0:T(8,128)(2,1)S(1)} async-done(((bf16[16,3,128,128]{3,2,1,0:T(8,128)(2,1)}), bf16[16,3,128,128]{3,2,1,0:T(8,128)(2,1)S(1)}, u32[]{:S(2)}, u32[]{:S(2)}) %all-to-all-start.2) | async-done | bytes 1572896 | tf_op jit(solution)/shard_map/all_to_all | solution.py:314
  50.7 6.7 %all-to-all-start = ((bf16[16,3,128,128]{3,2,1,0:T(8,128)(2,1)}), bf16[16,3,128,128]{3,2,1,0:T(8,128)(2,1)}, u32[]{:S(2)}, u32[]{:S(2)}) async-start(bf16[16,3,128,128]{3,2,1,0:T(8,128)(2,1)} %shard_map.46), calls=%async_computation | async-start | bytes 3145728 | tf_op jit(solution)/shard_map/all_to_all | solution.py:314
  63.7 32.6 %collective-permute-done.3.refs_3_ = bf16[192,256]{1,0:T(8,128)(2,1)S(1)} collective-permute-done((bf16[192,256]{1,0:T(8,128)(2,1)S(1)}, bf16[192,256]{1,0:T(8,128)(2,1)S(1)}, u32[]{:S(2)}, u32[]{:S(2)}) %collective-permute-start.3) | collective-permute-done | bytes 98336 | tf_op jit(solution)/shard_map/ppermute | solution.py:262
  96.3 2.6 %collective-permute-start.5 = (bf16[192,256]{1,0:T(8,128)(2,1)S(1)}, bf16[192,256]{1,0:T(8,128)(2,1)S(1)}, u32[]{:S(2)}, u32[]{:S(2)}) collective-permute-start(bf16[192,256]{1,0:T(8,128)(2,1)S(1)} %collective-permute-done.3.refs_3_), channel_id=1, source_target_pairs={{0,1},{1,2},{2,3},{3,4},{4,5},{5,6},{6,7},{7,0},{8,9},{9,10},{10,1... | collective-permute-start | bytes 294920 | tf_op jit(solution)/shard_map/ppermute | solution.py:262
  102.1 3.8 %collective-permute-done.7.refs_7_ = bf16[192,256]{1,0:T(8,128)(2,1)S(1)} collective-permute-done((bf16[192,256]{1,0:T(8,128)(2,1)S(1)}, bf16[192,256]{1,0:T(8,128)(2,1)S(1)}, u32[]{:S(2)}, u32[]{:S(2)}) %collective-permute-start.7) | collective-permute-done | bytes 98336 | tf_op jit(solution)/shard_map/ppermute | solution.py:262
  108.8 5.0 %collective-permute-done.8 = bf16[8,2,80,128]{3,2,1,0:T(8,128)(2,1)S(1)} collective-permute-done((bf16[8,2,80,128]{3,2,1,0:T(8,128)(2,1)S(1)}, bf16[8,2,80,128]{3,2,1,0:T(8,128)(2,1)S(1)}, u32[]{:S(2)}, u32[]{:S(2)}) %collective-permute-start.8) | collective-permute-done | bytes 327712 | tf_op jit(solution)/shard_map/ppermute | solution.py:262
  114.1 2.6 %collective-permute-start.15 = (bf16[8,2,112,128]{3,2,1,0:T(8,128)(2,1)S(1)}, bf16[8,2,112,128]{3,2,1,0:T(8,128)(2,1)S(1)}, u32[]{:S(2)}, u32[]{:S(2)}) collective-permute-start(bf16[8,2,112,128]{3,2,1,0:T(8,128)(2,1)S(1)} %get-tuple-element.34), channel_id=1, source_target_pairs={{8,128},{128,8},{136,0},{0,136},{9,129},{129,9},{137,1},{1,137},{1... | collective-permute-start | bytes 1376264 | tf_op jit(solution)/shard_map/ppermute | solution.py:270
  116.7 4.2 %collective-permute-done.10 = bf16[8,2,80,128]{3,2,1,0:T(8,128)(2,1)S(1)} collective-permute-done((bf16[8,2,80,128]{3,2,1,0:T(8,128)(2,1)S(1)}, bf16[8,2,80,128]{3,2,1,0:T(8,128)(2,1)S(1)}, u32[]{:S(2)}, u32[]{:S(2)}) %collective-permute-start.10) | collective-permute-done | bytes 327712 | tf_op jit(solution)/shard_map/ppermute | solution.py:262
  125.6 8.1 %shard_map.51 = bf16[16,128,128]{2,1,0:T(8,128)(2,1)} custom-call(bf16[16,3,128,128]{3,2,1,0:T(8,128)(2,1)S(1)} %copy-done.2, bf16[16,3,128,128]{3,2,1,0:T(8,128)(2,1)S(1)} %copy-done.2, bf16[16,3,128,128]{3,2,1,0:T(8,128)(2,1)S(1)} %copy-done.2), custom_call_target="tpu_custom_call" | custom-call | flops 2147483648 | bytes 2097152 | tf_op jit(solution)/shard_map/pallas_call | solution.py:76
  133.7 9.9 %all-to-all-start.3 = ((bf16[16,128,128]{2,1,0:T(8,128)(2,1)}), bf16[16,128,128]{2,1,0:T(8,128)(2,1)}, u32[]{:S(2)}, u32[]{:S(2)}) async-start(bf16[16,128,128]{2,1,0:T(8,128)(2,1)} %shard_map.51), calls=%async_computation.3 | async-start | bytes 1048576 | tf_op jit(solution)/shard_map/all_to_all | solution.py:314
  150.0 9.3 %shard_map.47 = bf16[16,128,128]{2,1,0:T(8,128)(2,1)} custom-call(bf16[16,3,128,128]{3,2,1,0:T(8,128)(2,1)} %all-to-all-done.q_ref.k_ref.v_ref, bf16[16,3,128,128]{3,2,1,0:T(8,128)(2,1)} %all-to-all-done.q_ref.k_ref.v_ref, bf16[16,3,128,128]{3,2,1,0:T(8,128)(2,1)} %all-to-all-done.q_ref.k_ref.v_ref), custom_call_target="tpu_custom_call" | custom-call | flops 2147483648 | bytes 2097152 | tf_op jit(solution)/shard_map/pallas_call | solution.py:76
  159.3 6.5 %all-to-all-start.1 = ((bf16[16,128,128]{2,1,0:T(8,128)(2,1)}), bf16[16,128,128]{2,1,0:T(8,128)(2,1)}, u32[]{:S(2)}, u32[]{:S(2)}) async-start(bf16[16,128,128]{2,1,0:T(8,128)(2,1)} %shard_map.47), calls=%async_computation.1 | async-start | bytes 1048576 | tf_op jit(solution)/shard_map/all_to_all | solution.py:314
  165.9 2.8 %collective-permute-start.13 = (bf16[4,8,2,80,128]{4,3,2,1,0:T(8,128)(2,1)}, bf16[4,8,2,80,128]{4,3,2,1,0:T(8,128)(2,1)}, u32[]{:S(2)}, u32[]{:S(2)}) collective-permute-start(bf16[4,8,2,80,128]{4,3,2,1,0:T(8,128)(2,1)} %collective-permute-done.11.refs_2_), channel_id=1, source_target_pairs={{8,128},{128,8},{136,0},{0,136},{9,129},{129,9},{137,1},{1,137},{1... | collective-permute-start | bytes 3932168 | tf_op jit(solution)/shard_map/ppermute | solution.py:270
  168.9 7.1 %collective-permute-done.20.refs_10_ = bf16[2,8,2,112,128]{4,3,2,1,0:T(8,128)(2,1)} collective-permute-done((bf16[2,8,2,112,128]{4,3,2,1,0:T(8,128)(2,1)S(1)}, bf16[2,8,2,112,128]{4,3,2,1,0:T(8,128)(2,1)}, u32[]{:S(2)}, u32[]{:S(2)}) %collective-permute-start.20) | collective-permute-done | bytes 917536 | tf_op jit(solution)/shard_map/ppermute | solution.py:262
  176.0 3.2 %collective-permute-start.22 = (bf16[2,8,2,112,128]{4,3,2,1,0:T(8,128)(2,1)}, bf16[2,8,2,112,128]{4,3,2,1,0:T(8,128)(2,1)}, u32[]{:S(2)}, u32[]{:S(2)}) collective-permute-start(bf16[2,8,2,112,128]{4,3,2,1,0:T(8,128)(2,1)} %collective-permute-done.20.refs_10_), channel_id=1, source_target_pairs={{0,96},{32,0},{64,32},{96,64},{1,97},{33,1},{65,33},{97,65},{2,98}... | collective-permute-start | bytes 2752520 | tf_op jit(solution)/shard_map/ppermute | solution.py:262
  179.2 15.5 %collective-permute-start.23 = (bf16[16,128,128]{2,1,0:T(8,128)(2,1)}, bf16[16,128,128]{2,1,0:T(8,128)(2,1)}, u32[]{:S(2)}, u32[]{:S(2)}) collective-permute-start(bf16[16,128,128]{2,1,0:T(8,128)(2,1)} %all-to-all-done.3.refs_0_.a_ref), channel_id=1, source_target_pairs={{0,16},{16,0},{1,17},{17,1},{2,18},{18,2},{3,19},{19,3},{4,20},{20... | collective-permute-start | bytes 1572872 | tf_op jit(solution)/shard_map/ppermute | solution.py:274
  195.6 4.1 %collective-permute-done.13.refs_4_ = bf16[4,8,2,80,128]{4,3,2,1,0:T(8,128)(2,1)} collective-permute-done((bf16[4,8,2,80,128]{4,3,2,1,0:T(8,128)(2,1)}, bf16[4,8,2,80,128]{4,3,2,1,0:T(8,128)(2,1)}, u32[]{:S(2)}, u32[]{:S(2)}) %collective-permute-start.13) | collective-permute-done | bytes 1310752 | tf_op jit(solution)/shard_map/ppermute | solution.py:270
  202.2 2.5 %shard_map.49 = (bf16[4,8,80,128]{3,2,1,0:T(8,128)(2,1)S(1)}, bf16[4,8,80,128]{3,2,1,0:T(8,128)(2,1)S(1)}, bf16[4,8,80,128]{3,2,1,0:T(8,128)(2,1)S(1)}, bf16[4,8...) custom-call(bf16[16,128,128]{2,1,0:T(8,128)(2,1)} %all-to-all-done.1, ...), custom_call_target="tpu_custom_call" | custom-call | bytes 8388608 | tf_op jit(solution)/shard_map/pallas_call | solution.py:140
  204.7 4.9 %shard_map.53.refs_12_ = f32[2,4,192,256]{3,2,1,0:T(8,128)} custom-call(s32[5]{0:T(128)S(1)} %stack.56.pos_ref, bf16[16,128,128]{2,1,0:T(8,128)(2,1)} %all-to-all-done.3.refs_0_.a_ref, bf16[16,128,128]{2,1,0:T(8,128)(2,1)} %collective-permute-done.23.b_ref, bf16[4,8,80,128]{3,2,1,0:T(8,128)(2,1)S(1)} %get-tuple-element.47.refs_0_, ...), custom_call_target="tpu_custom_call" | custom-call | flops 1610612736 | bytes 9437184 | tf_op jit(solution)/shard_map/pallas_call | solution.py:199
  211.1 3.7 %shard_map.54 = (bf16[2,4,192,128]{3,2,1,0:T(8,128)(2,1)S(1)}, bf16[2,4,192,128]{3,2,1,0:T(8,128)(2,1)S(1)}) custom-call(s32[5]{0:T(128)S(1)} %stack.56.pos_ref, bf16[16,128,128]{2,1,0:T(8,128)(2,1)} %all-to-all-done.1.refs_0_.a_ref, bf16[16,128,128]{2,1,0:T(8,128)(2,1)} %collective-permute-done.b_ref, ...), custom_call_target="tpu_custom_call" | custom-call | flops 1610612736 | bytes 9437184 | tf_op jit(solution)/shard_map/pallas_call | solution.py:199
  214.8 9.7 %collective-permute-start.24 = (bf16[2,4,192,128]{3,2,1,0:T(8,128)(2,1)S(1)}, bf16[2,4,192,128]{3,2,1,0:T(8,128)(2,1)S(1)}, u32[]{:S(2)}, u32[]{:S(2)}) collective-permute-start(bf16[2,4,192,128]{3,2,1,0:T(8,128)(2,1)S(1)} %get-tuple-element.60), channel_id=1, source_target_pairs={{0,16},{16,0},{1,17},{17,1},{2,18},{18,2},{3,19},{19,3},{4,20},{20... | collective-permute-start | bytes 1179656 | tf_op jit(solution)/shard_map/ppermute | solution.py:274
  (58 shorter events, 33.4 us)
Async XLA Ops:
  3.0 46.5 %all-to-all-start.2 = ((bf16[16,3,128,128]{3,2,1,0:T(8,128)(2,1)}), bf16[16,3,128,128]{3,2,1,0:T(8,128)(2,1)S(1)}, u32[]{:S(2)}, u32[]{:S(2)}) async-start(bf16[16,3,128,128]{3,2,1,0:T(8,128)(2,1)} %shard_map.50), calls=%async_computation.2 | async-start | bytes 3145728 | tf_op jit(solution)/shard_map/all_to_all | solution.py:314
  50.7 83.1 %all-to-all-start = ((bf16[16,3,128,128]{3,2,1,0:T(8,128)(2,1)}), bf16[16,3,128,128]{3,2,1,0:T(8,128)(2,1)}, u32[]{:S(2)}, u32[]{:S(2)}) async-start(bf16[16,3,128,128]{3,2,1,0:T(8,128)(2,1)} %shard_map.46), calls=%async_computation | async-start | bytes 3145728 | tf_op jit(solution)/shard_map/all_to_all | solution.py:314
  57.3 39.0 %collective-permute-start.3 = (bf16[192,256]{1,0:T(8,128)(2,1)S(1)}, bf16[192,256]{1,0:T(8,128)(2,1)S(1)}, u32[]{:S(2)}, u32[]{:S(2)}) collective-permute-start(bf16[192,256]{1,0:T(8,128)(2,1)S(1)} %bitcast.20), channel_id=1, source_target_pairs={{0,2},{1,3},{2,4},{3,5},{4,6},{5,7},{6,0},{7,1},{8,10},{9,11},{10,... | collective-permute-start | bytes 294920 | tf_op jit(solution)/shard_map/ppermute | solution.py:262
  59.6 40.5 %collective-permute-start.4 = (bf16[192,256]{1,0:T(8,128)(2,1)S(1)}, bf16[192,256]{1,0:T(8,128)(2,1)S(1)}, u32[]{:S(2)}, u32[]{:S(2)}) collective-permute-start(bf16[192,256]{1,0:T(8,128)(2,1)S(1)} %bitcast.21), channel_id=1, source_target_pairs={{0,6},{1,7},{2,0},{3,1},{4,2},{5,3},{6,4},{7,5},{8,14},{9,15},{10,... | collective-permute-start | bytes 294920 | tf_op jit(solution)/shard_map/ppermute | solution.py:262
  61.0 40.3 %collective-permute-start.1 = (bf16[192,256]{1,0:T(8,128)(2,1)S(1)}, bf16[192,256]{1,0:T(8,128)(2,1)S(1)}, u32[]{:S(2)}, u32[]{:S(2)}) collective-permute-start(bf16[192,256]{1,0:T(8,128)(2,1)S(1)} %bitcast.22), channel_id=1, source_target_pairs={{0,1},{1,2},{2,3},{3,4},{4,5},{5,6},{6,7},{7,0},{8,9},{9,10},{10,1... | collective-permute-start | bytes 294920 | tf_op jit(solution)/shard_map/ppermute | solution.py:262
  62.3 39.0 %collective-permute-start.2 = (bf16[192,256]{1,0:T(8,128)(2,1)S(1)}, bf16[192,256]{1,0:T(8,128)(2,1)S(1)}, u32[]{:S(2)}, u32[]{:S(2)}) collective-permute-start(bf16[192,256]{1,0:T(8,128)(2,1)S(1)} %bitcast.23), channel_id=1, source_target_pairs={{0,7},{1,0},{2,1},{3,2},{4,3},{5,4},{6,5},{7,6},{8,15},{9,8},{10,9... | collective-permute-start | bytes 294920 | tf_op jit(solution)/shard_map/ppermute | solution.py:262
  106.0 7.8 %collective-permute-start.8 = (bf16[8,2,80,128]{3,2,1,0:T(8,128)(2,1)S(1)}, bf16[8,2,80,128]{3,2,1,0:T(8,128)(2,1)S(1)}, u32[]{:S(2)}, u32[]{:S(2)}) collective-permute-start(bf16[8,2,80,128]{3,2,1,0:T(8,128)(2,1)S(1)} %get-tuple-element.33), channel_id=1, source_target_pairs={{0,32},{32,64},{64,96},{96,0},{1,33},{33,65},{65,97},{97,1},{2,34}... | collective-permute-start | bytes 983048 | tf_op jit(solution)/shard_map/ppermute | solution.py:262
  107.3 9.4 %collective-permute-start.9 = (bf16[8,2,80,128]{3,2,1,0:T(8,128)(2,1)S(1)}, bf16[8,2,80,128]{3,2,1,0:T(8,128)(2,1)S(1)}, u32[]{:S(2)}, u32[]{:S(2)}) collective-permute-start(bf16[8,2,80,128]{3,2,1,0:T(8,128)(2,1)S(1)} %get-tuple-element.33), channel_id=1, source_target_pairs={{0,96},{32,0},{64,32},{96,64},{1,97},{33,1},{65,33},{97,65},{2,98}... | collective-permute-start | bytes 983048 | tf_op jit(solution)/shard_map/ppermute | solution.py:262
  114.1 31.3 %collective-permute-start.15 = (bf16[8,2,112,128]{3,2,1,0:T(8,128)(2,1)S(1)}, bf16[8,2,112,128]{3,2,1,0:T(8,128)(2,1)S(1)}, u32[]{:S(2)}, u32[]{:S(2)}) collective-permute-start(bf16[8,2,112,128]{3,2,1,0:T(8,128)(2,1)S(1)} %get-tuple-element.34), channel_id=1, source_target_pairs={{8,128},{128,8},{136,0},{0,136},{9,129},{129,9},{137,1},{1,137},{1... | collective-permute-start | bytes 1376264 | tf_op jit(solution)/shard_map/ppermute | solution.py:270
  121.1 44.8 %collective-permute-start.11 = (bf16[4,8,2,80,128]{4,3,2,1,0:T(8,128)(2,1)S(1)}, bf16[4,8,2,80,128]{4,3,2,1,0:T(8,128)(2,1)}, u32[]{:S(2)}, u32[]{:S(2)}) collective-permute-start(bf16[4,8,2,80,128]{4,3,2,1,0:T(8,128)(2,1)S(1)} %pad_maximum_fusion.refs_1_), channel_id=1, source_target_pairs={{0,8},{8,0},{1,9},{9,1},{2,10},{10,2},{3,11},{11,3},{4,12},{12,4},... | collective-permute-start | bytes 3932168 | tf_op jit(solution)/shard_map/ppermute | solution.py:266
  122.7 27.0 %collective-permute-start.17 = (bf16[2,8,2,112,128]{4,3,2,1,0:T(8,128)(2,1)S(1)}, bf16[2,8,2,112,128]{4,3,2,1,0:T(8,128)(2,1)}, u32[]{:S(2)}, u32[]{:S(2)}) collective-permute-start(bf16[2,8,2,112,128]{4,3,2,1,0:T(8,128)(2,1)S(1)} %pad_maximum_fusion.1.refs_5_), channel_id=1, source_target_pairs={{0,32},{32,64},{64,96},{96,0},{1,33},{33,65},{65,97},{97,1},{2,34}... | collective-permute-start | bytes 2752520 | tf_op jit(solution)/shard_map/ppermute | solution.py:262
  123.8 21.6 %collective-permute-start.16 = (bf16[8,2,112,128]{3,2,1,0:T(8,128)(2,1)}, bf16[8,2,112,128]{3,2,1,0:T(8,128)(2,1)}, u32[]{:S(2)}, u32[]{:S(2)}) collective-permute-start(bf16[8,2,112,128]{3,2,1,0:T(8,128)(2,1)} %collective-permute-done.14), channel_id=1, source_target_pairs={{8,128},{128,8},{136,0},{0,136},{9,129},{129,9},{137,1},{1,137},{1... | collective-permute-start | bytes 1376264 | tf_op jit(solution)/shard_map/ppermute | solution.py:270
  133.7 25.6 %all-to-all-start.3 = ((bf16[16,128,128]{2,1,0:T(8,128)(2,1)}), bf16[16,128,128]{2,1,0:T(8,128)(2,1)}, u32[]{:S(2)}, u32[]{:S(2)}) async-start(bf16[16,128,128]{2,1,0:T(8,128)(2,1)} %shard_map.51), calls=%async_computation.3 | async-start | bytes 1048576 | tf_op jit(solution)/shard_map/all_to_all | solution.py:314
  143.6 25.1 %collective-permute-start.19 = (bf16[2,8,2,112,128]{4,3,2,1,0:T(8,128)(2,1)S(1)}, bf16[2,8,2,112,128]{4,3,2,1,0:T(8,128)(2,1)}, u32[]{:S(2)}, u32[]{:S(2)}) collective-permute-start(bf16[2,8,2,112,128]{4,3,2,1,0:T(8,128)(2,1)S(1)} %pad_maximum_fusion.1.refs_5_), channel_id=1, source_target_pairs={{0,96},{32,0},{64,32},{96,64},{1,97},{33,1},{65,33},{97,65},{2,98}... | collective-permute-start | bytes 2752520 | tf_op jit(solution)/shard_map/ppermute | solution.py:262
  147.4 28.6 %collective-permute-start.20 = (bf16[2,8,2,112,128]{4,3,2,1,0:T(8,128)(2,1)S(1)}, bf16[2,8,2,112,128]{4,3,2,1,0:T(8,128)(2,1)}, u32[]{:S(2)}, u32[]{:S(2)}) collective-permute-start(bf16[2,8,2,112,128]{4,3,2,1,0:T(8,128)(2,1)S(1)} %pad_maximum_fusion.2.refs_6_), channel_id=1, source_target_pairs={{0,96},{32,0},{64,32},{96,64},{1,97},{33,1},{65,33},{97,65},{2,98}... | collective-permute-start | bytes 2752520 | tf_op jit(solution)/shard_map/ppermute | solution.py:262
  148.7 46.1 %collective-permute-start.12 = (bf16[4,8,2,80,128]{4,3,2,1,0:T(8,128)(2,1)S(1)}, bf16[4,8,2,80,128]{4,3,2,1,0:T(8,128)(2,1)}, u32[]{:S(2)}, u32[]{:S(2)}) collective-permute-start(bf16[4,8,2,80,128]{4,3,2,1,0:T(8,128)(2,1)S(1)} %pad_maximum_fusion.refs_1_), channel_id=1, source_target_pairs={{8,128},{128,8},{136,0},{0,136},{9,129},{129,9},{137,1},{1,137},{1... | collective-permute-start | bytes 3932168 | tf_op jit(solution)/shard_map/ppermute | solution.py:270
  149.7 29.5 %collective-permute-start.18 = (bf16[2,8,2,112,128]{4,3,2,1,0:T(8,128)(2,1)S(1)}, bf16[2,8,2,112,128]{4,3,2,1,0:T(8,128)(2,1)}, u32[]{:S(2)}, u32[]{:S(2)}) collective-permute-start(bf16[2,8,2,112,128]{4,3,2,1,0:T(8,128)(2,1)S(1)} %pad_maximum_fusion.2.refs_6_), channel_id=1, source_target_pairs={{0,32},{32,64},{64,96},{96,0},{1,33},{33,65},{65,97},{97,1},{2,34}... | collective-permute-start | bytes 2752520 | tf_op jit(solution)/shard_map/ppermute | solution.py:262
  159.3 35.4 %all-to-all-start.1 = ((bf16[16,128,128]{2,1,0:T(8,128)(2,1)}), bf16[16,128,128]{2,1,0:T(8,128)(2,1)}, u32[]{:S(2)}, u32[]{:S(2)}) async-start(bf16[16,128,128]{2,1,0:T(8,128)(2,1)} %shard_map.47), calls=%async_computation.1 | async-start | bytes 1048576 | tf_op jit(solution)/shard_map/all_to_all | solution.py:314
  165.9 33.9 %collective-permute-start.13 = (bf16[4,8,2,80,128]{4,3,2,1,0:T(8,128)(2,1)}, bf16[4,8,2,80,128]{4,3,2,1,0:T(8,128)(2,1)}, u32[]{:S(2)}, u32[]{:S(2)}) collective-permute-start(bf16[4,8,2,80,128]{4,3,2,1,0:T(8,128)(2,1)} %collective-permute-done.11.refs_2_), channel_id=1, source_target_pairs={{8,128},{128,8},{136,0},{0,136},{9,129},{129,9},{137,1},{1,137},{1... | collective-permute-start | bytes 3932168 | tf_op jit(solution)/shard_map/ppermute | solution.py:270
  168.7 26.5 %collective-permute-start.21 = (bf16[2,8,2,112,128]{4,3,2,1,0:T(8,128)(2,1)}, bf16[2,8,2,112,128]{4,3,2,1,0:T(8,128)(2,1)}, u32[]{:S(2)}, u32[]{:S(2)}) collective-permute-start(bf16[2,8,2,112,128]{4,3,2,1,0:T(8,128)(2,1)} %collective-permute-done.17.refs_7_), channel_id=1, source_target_pairs={{0,32},{32,64},{64,96},{96,0},{1,33},{33,65},{65,97},{97,1},{2,34}... | collective-permute-start | bytes 2752520 | tf_op jit(solution)/shard_map/ppermute | solution.py:262
  176.0 19.7 %collective-permute-start.22 = (bf16[2,8,2,112,128]{4,3,2,1,0:T(8,128)(2,1)}, bf16[2,8,2,112,128]{4,3,2,1,0:T(8,128)(2,1)}, u32[]{:S(2)}, u32[]{:S(2)}) collective-permute-start(bf16[2,8,2,112,128]{4,3,2,1,0:T(8,128)(2,1)} %collective-permute-done.20.refs_10_), channel_id=1, source_target_pairs={{0,96},{32,0},{64,32},{96,64},{1,97},{33,1},{65,33},{97,65},{2,98}... | collective-permute-start | bytes 2752520 | tf_op jit(solution)/shard_map/ppermute | solution.py:262
  179.2 25.5 %collective-permute-start.23 = (bf16[16,128,128]{2,1,0:T(8,128)(2,1)}, bf16[16,128,128]{2,1,0:T(8,128)(2,1)}, u32[]{:S(2)}, u32[]{:S(2)}) collective-permute-start(bf16[16,128,128]{2,1,0:T(8,128)(2,1)} %all-to-all-done.3.refs_0_.a_ref), channel_id=1, source_target_pairs={{0,16},{16,0},{1,17},{17,1},{2,18},{18,2},{3,19},{19,3},{4,20},{20... | collective-permute-start | bytes 1572872 | tf_op jit(solution)/shard_map/ppermute | solution.py:274
  194.8 14.9 %collective-permute-start = (bf16[16,128,128]{2,1,0:T(8,128)(2,1)}, bf16[16,128,128]{2,1,0:T(8,128)(2,1)}, u32[]{:S(2)}, u32[]{:S(2)}) collective-permute-start(bf16[16,128,128]{2,1,0:T(8,128)(2,1)} %all-to-all-done.1.refs_0_.a_ref), channel_id=1, source_target_pairs={{0,16},{16,0},{1,17},{17,1},{2,18},{18,2},{3,19},{19,3},{4,20},{20... | collective-permute-start | bytes 1572872 | tf_op jit(solution)/shard_map/ppermute | solution.py:274
  214.8 11.0 %collective-permute-start.24 = (bf16[2,4,192,128]{3,2,1,0:T(8,128)(2,1)S(1)}, bf16[2,4,192,128]{3,2,1,0:T(8,128)(2,1)S(1)}, u32[]{:S(2)}, u32[]{:S(2)}) collective-permute-start(bf16[2,4,192,128]{3,2,1,0:T(8,128)(2,1)S(1)} %get-tuple-element.60), channel_id=1, source_target_pairs={{0,16},{16,0},{1,17},{17,1},{2,18},{18,2},{3,19},{19,3},{4,20},{20... | collective-permute-start | bytes 1179656 | tf_op jit(solution)/shard_map/ppermute | solution.py:274
  (10 other events, 82.5 us)

commit v2 on v1

--- a/solution.py
+++ b/solution.py
@@ -21,69 +21,80 @@
     return pl.CostEstimate(flops=flops, bytes_accessed=nbytes, transcendentals=exps)
 
 
-def pack_kernel(head, q_ref, k_ref, v_ref, out_ref, sem):
-    copies = [
-        pltpu.make_async_copy(
-            ref.at[:, pl.ds(group * 256 + head * HEAD_DIM, HEAD_DIM)],
-            out_ref.at[group, index],
-            sem.at[group, index],
-        )
+def pack_kernel(head, q_ref, k_ref, v_ref, out_ref, stage, in_sem, out_sem):
+    loads = [
+        [
+            pltpu.make_async_copy(
+                ref.at[:, pl.ds(group * 256 + head * HEAD_DIM, HEAD_DIM)],
+                stage.at[group, index],
+                in_sem.at[group, index],
+            )
+            for index, ref in enumerate((q_ref, k_ref, v_ref))
+        ]
         for group in range(16)
-        for index, ref in enumerate((q_ref, k_ref, v_ref))
-    ]
-    for copy in copies:
-        copy.start()
-    for copy in copies:
-        copy.wait()
+    ]
+    stores = [
+        pltpu.make_async_copy(stage.at[group], out_ref.at[group], out_sem.at[group])
+        for group in range(16)
+    ]
+    for group in loads:
+        for copy in group:
+            copy.start()
+    for group, store in zip(loads, stores):
+        for copy in group:
+            copy.wait()
+        store.start()
+    for store in stores:
+        store.wait()
 
 
 def pack(queries, key_rows, value_rows, head):
-    tokens = queries.shape[0]
+    shape = (16, 3, queries.shape[0], HEAD_DIM)
     return pl.pallas_call(
         functools.partial(pack_kernel, head),
         in_specs=[pl.BlockSpec(memory_space=pltpu.HBM)] * 3,
-        out_shape=pltpu.HBM((16, 3, tokens, HEAD_DIM), BF16),
-        scratch_shapes=[pltpu.SemaphoreType.DMA((16, 3))],
+        out_specs=pl.BlockSpec(memory_space=pltpu.HBM),
+        out_shape=pltpu.HBM(shape, BF16),
+        scratch_shapes=[
+            pltpu.VMEM(shape, BF16),
+            pltpu.SemaphoreType.DMA((16, 3)),
+            pltpu.SemaphoreType.DMA((16,)),
+        ],
         compiler_params=pltpu.CompilerParams(vmem_limit_bytes=60 * 1024 * 1024),
         cost_estimate=cost(0, 5 << 20),
     )(queries, key_rows, value_rows)
 
 
-def attend_rows(rows, keys, values):
-    scores = lax.dot_general(
-        rows, keys, (((1,), (1,)), ((), ())), preferred_element_type=F32
-    )
-    largest = jnp.max(scores, axis=1, keepdims=True)
-    weights = jnp.exp2((scores - largest) * SCALE)
-    total = jnp.sum(weights, axis=1, keepdims=True)
-    mixed = jnp.dot(weights.astype(BF16), values, preferred_element_type=F32)
-    return (mixed / total).astype(BF16)
-
-
 def attend_kernel(sub, q_ref, k_ref, v_ref, o_ref):
     keys = k_ref[:, 0].reshape(-1, HEAD_DIM)
     values = v_ref[:, 0].reshape(-1, HEAD_DIM)
+    values = jnp.concatenate([values, jnp.ones_like(values)], axis=1)
     rows = q_ref[:, 0].reshape(-1, HEAD_DIM)
-    pieces = [
-        attend_rows(rows[low : low + sub], keys, values) for low in range(0, rows.shape[0], sub)
-    ]
+    pieces = []
+    for low in range(0, rows.shape[0], sub):
+        scores = lax.dot_general(
+            rows[low : low + sub], keys, (((1,), (1,)), ((), ())), preferred_element_type=F32
+        )
+        largest = jnp.max(scores, axis=1, keepdims=True)
+        weights = jnp.exp2((scores - largest) * SCALE).astype(BF16)
+        mixed = jnp.dot(weights, values, preferred_element_type=F32)
+        pieces.append((mixed[:, :HEAD_DIM] / mixed[:, HEAD_DIM:]).astype(BF16))
     o_ref[...] = jnp.concatenate(pieces, 0).reshape(o_ref.shape)
 
 
 def attend(arrived):
     n, _, tokens, _ = arrived.shape
-    per = 4
+
+    def part(index):
+        return pl.BlockSpec((n, 1, tokens, HEAD_DIM), lambda i: (0, index, 0, 0))
+
     return pl.pallas_call(
         functools.partial(attend_kernel, 256),
-        grid=(n // per,),
-        in_specs=[
-            pl.BlockSpec((per, 1, tokens, HEAD_DIM), lambda i: (i, 0, 0, 0)),
-            pl.BlockSpec((n, 1, tokens, HEAD_DIM), lambda i: (0, 1, 0, 0)),
-            pl.BlockSpec((n, 1, tokens, HEAD_DIM), lambda i: (0, 2, 0, 0)),
-        ],
-        out_specs=pl.BlockSpec((per, tokens, HEAD_DIM), lambda i: (i, 0, 0)),
+        grid=(1,),
+        in_specs=[part(0), part(1), part(2)],
+        out_specs=pl.BlockSpec((n, tokens, HEAD_DIM), lambda i: (0, 0, 0)),
         out_shape=pltpu.HBM((n, tokens, HEAD_DIM), BF16),
-        compiler_params=pltpu.CompilerParams(vmem_limit_bytes=24 << 20),
+        compiler_params=pltpu.CompilerParams(vmem_limit_bytes=40 << 20),
         cost_estimate=cost(4 * 2048 * 2048 * 128, 2 << 20, 2048 * 2048),
     )(arrived, arrived, arrived)
 
@@ -92,7 +103,7 @@
 FAR = (-3, 3, -4)
 Z_OFFSETS = NEAR + FAR
 X_OFFSETS = (0, -1, 1, 2)
-ROWS_A, ROWS_B = 80, 112
+ROWS_A, ROWS_B = 64, 128
 
 
 def gather_features(pos_ref, features, a_rel):
@@ -305,8 +316,9 @@
     a_pair, a_cross = pair_swap(a), cross_swap(a)
     up.append(shift(far, "x", 4, 1))
     down.append(shift(far, "x", 4, -1))
+    up_last = shift(up[0], "x", 4, 1)
     a_far = cross_swap(a_pair)
-    last = [shift(up[0], "x", 4, 1), shift(down[1], "x", 4, -1)]
+    last = [up_last, shift(down[1], "x", 4, -1)]
     return (a, a_pair, a_cross, a_far, near, far, *up, *down, *last)
 
 

time: 229 us -> 232 us (1.013)
  waiting for transfers between devices: 92.9 us -> 105 us
  Pallas kernels: 39.2 us -> 33.5 us
  starting transfers between devices: 89.6 us -> 85.4 us
    ppermute x16, waiting for transfers between devices: 54.1 us -> 68.5 us  [shift(): lax.ppermute(value, axis, [(i, (i + step) % size) for i in range(size)])]
    pallas_call x2, Pallas kernels: 17.5 us -> 12.4 us  [attend(): pl.pallas_call(functools.partial(attend_kernel, 256), grid=(1,), in_specs...]
    ppermute x4, waiting for transfers between devices: 4.09 us -> 0.01 us  [cross_swap(): return lax.ppermute(value, ('yh', 'yl'), [(1, 2), (2, 1), (3, 0), (0, 3)])]
    ppermute x4, starting transfers between devices: 8.22 us -> 5.58 us  [cross_swap(): return lax.ppermute(value, ('yh', 'yl'), [(1, 2), (2, 1), (3, 0), (0, 3)])]
    ppermute x3, starting transfers between devices: 25.5 us -> 23 us  [core_swap(): return lax.ppermute(value, 'core', [(0, 1), (1, 0)])]
  transfers between devices with their start and end apart: 29 -> 29, of which waited for: 10 -> 11; matrix products, arithmetic and copies ran while one was open for 1% -> 1% of each run, Pallas kernels for 13% -> 11%
where the time goes in v2:
time: 232 us; the launch traced here: 231 us
  waiting for transfers between devices  105 us (45%)
  starting transfers between devices  85.4 us (37%)
  Pallas kernels  33.5 us (14%)
  local copies, waits for them, and re-layouts  3.86 us (2%)
  other arithmetic  2.57 us (1%)
    ppermute x16, waiting for transfers between devices, shift(): lax.ppermute(value, axis, [(i, (i + step) % size) for i in range(size)])  68.5 us
    all_to_all x4, waiting for transfers between devices, all_to_all(): return lax.all_to_all(value, SEQ, 0, 0, tiled=True)  33.7 us
    all_to_all x4, starting transfers between devices, all_to_all(): return lax.all_to_all(value, SEQ, 0, 0, tiled=True)  33 us
    ppermute x3, starting transfers between devices, core_swap(): return lax.ppermute(value, 'core', [(0, 1), (1, 0)])  23 us
    ppermute x16, starting transfers between devices, shift(): lax.ppermute(value, axis, [(i, (i + step) % size) for i in range(size)])  22.3 us
    pallas_call x2, Pallas kernels, attend(): pl.pallas_call(functools.partial(attend_kernel, 256), grid=(1,), in_specs...  12.4 us
    pallas_call x2, Pallas kernels, project(): pl.pallas_call(functools.partial(project_kernel, head), grid_spec=pltpu.P...  8.62 us
    ppermute x4, starting transfers between devices, cross_swap(): return lax.ppermute(value, ('yh', 'yl'), [(1, 2), (2, 1), (3, 0), (0, 3)])  5.58 us
  transfers between devices with their start and end apart: 29, of which 11 were waited for; matrix products, arithmetic and copies ran while one was open for 1% of the time, Pallas kernels for 11%

profile of v2, /device:TPU:1, one launch (start us, length us, event | category | flops | bytes accessed | tf_op | source)
XLA Modules:
  0.0 230.6 jit_solution(15174229412691955846)
XLA Ops:
  0.0 2.6 %shard_map.50 = bf16[16,3,128,128]{3,2,1,0:T(8,128)(2,1)} custom-call(bf16[128,4096]{1,0:T(8,128)(2,1)} %bitcast.25, bf16[128,4096]{1,0:T(8,128)(2,1)} %bitcast.27, bf16[128,4096]{1,0:T(8,128)(2,1)} %bitcast.29), custom_call_target="tpu_custom_call" | custom-call | bytes 5242880 | tf_op jit(solution)/shard_map/pallas_call | solution.py:53
  2.6 10.1 %all-to-all-start.2 = ((bf16[16,3,128,128]{3,2,1,0:T(8,128)(2,1)}), bf16[16,3,128,128]{3,2,1,0:T(8,128)(2,1)S(1)}, u32[]{:S(2)}, u32[]{:S(2)}) async-start(bf16[16,3,128,128]{3,2,1,0:T(8,128)(2,1)} %shard_map.50), calls=%async_computation.2 | async-start | bytes 3145728 | tf_op jit(solution)/shard_map/all_to_all | solution.py:326
  12.8 2.6 %shard_map.46 = bf16[16,3,128,128]{3,2,1,0:T(8,128)(2,1)} custom-call(bf16[128,4096]{1,0:T(8,128)(2,1)} %bitcast.26, bf16[128,4096]{1,0:T(8,128)(2,1)} %bitcast.28, bf16[128,4096]{1,0:T(8,128)(2,1)} %bitcast.30), custom_call_target="tpu_custom_call" | custom-call | bytes 5242880 | tf_op jit(solution)/shard_map/pallas_call | solution.py:53
  15.4 33.7 %all-to-all-done.2.q_ref.k_ref.v_ref = bf16[16,3,128,128]{3,2,1,0:T(8,128)(2,1)S(1)} async-done(((bf16[16,3,128,128]{3,2,1,0:T(8,128)(2,1)}), bf16[16,3,128,128]{3,2,1,0:T(8,128)(2,1)S(1)}, u32[]{:S(2)}, u32[]{:S(2)}) %all-to-all-start.2) | async-done | bytes 1572896 | tf_op jit(solution)/shard_map/all_to_all | solution.py:326
  50.3 6.6 %all-to-all-start = ((bf16[16,3,128,128]{3,2,1,0:T(8,128)(2,1)}), bf16[16,3,128,128]{3,2,1,0:T(8,128)(2,1)S(1)}, u32[]{:S(2)}, u32[]{:S(2)}) async-start(bf16[16,3,128,128]{3,2,1,0:T(8,128)(2,1)} %shard_map.46), calls=%async_computation | async-start | bytes 3145728 | tf_op jit(solution)/shard_map/all_to_all | solution.py:326
  56.9 2.3 %collective-permute-start.3 = (bf16[192,256]{1,0:T(8,128)(2,1)S(1)}, bf16[192,256]{1,0:T(8,128)(2,1)S(1)}, u32[]{:S(2)}, u32[]{:S(2)}) collective-permute-start(bf16[192,256]{1,0:T(8,128)(2,1)S(1)} %bitcast.20), channel_id=1, source_target_pairs={{0,2},{1,3},{2,4},{3,5},{4,6},{5,7},{6,0},{7,1},{8,10},{9,11},{10,... | collective-permute-start | bytes 294920 | tf_op jit(solution)/shard_map/ppermute | solution.py:273
  63.3 32.6 %collective-permute-done.3.refs_3_ = bf16[192,256]{1,0:T(8,128)(2,1)S(1)} collective-permute-done((bf16[192,256]{1,0:T(8,128)(2,1)S(1)}, bf16[192,256]{1,0:T(8,128)(2,1)S(1)}, u32[]{:S(2)}, u32[]{:S(2)}) %collective-permute-start.3) | collective-permute-done | bytes 98336 | tf_op jit(solution)/shard_map/ppermute | solution.py:273
  95.8 2.6 %collective-permute-start.5 = (bf16[192,256]{1,0:T(8,128)(2,1)S(1)}, bf16[192,256]{1,0:T(8,128)(2,1)S(1)}, u32[]{:S(2)}, u32[]{:S(2)}) collective-permute-start(bf16[192,256]{1,0:T(8,128)(2,1)S(1)} %collective-permute-done.3.refs_3_), channel_id=1, source_target_pairs={{0,1},{1,2},{2,3},{3,4},{4,5},{5,6},{6,7},{7,0},{8,9},{9,10},{10,1... | collective-permute-start | bytes 294920 | tf_op jit(solution)/shard_map/ppermute | solution.py:273
  101.7 3.6 %collective-permute-done.7.refs_7_ = bf16[192,256]{1,0:T(8,128)(2,1)S(1)} collective-permute-done((bf16[192,256]{1,0:T(8,128)(2,1)S(1)}, bf16[192,256]{1,0:T(8,128)(2,1)S(1)}, u32[]{:S(2)}, u32[]{:S(2)}) %collective-permute-start.7) | collective-permute-done | bytes 98336 | tf_op jit(solution)/shard_map/ppermute | solution.py:273
  109.1 3.8 %collective-permute-done.8 = bf16[8,2,64,128]{3,2,1,0:T(8,128)(2,1)S(1)} collective-permute-done((bf16[8,2,64,128]{3,2,1,0:T(8,128)(2,1)S(1)}, bf16[8,2,64,128]{3,2,1,0:T(8,128)(2,1)S(1)}, u32[]{:S(2)}, u32[]{:S(2)}) %collective-permute-start.8) | collective-permute-done | bytes 262176 | tf_op jit(solution)/shard_map/ppermute | solution.py:273
  120.4 6.2 %shard_map.51 = bf16[16,128,128]{2,1,0:T(8,128)(2,1)} custom-call(bf16[16,3,128,128]{3,2,1,0:T(8,128)(2,1)S(1)} %copy-done.4, bf16[16,3,128,128]{3,2,1,0:T(8,128)(2,1)S(1)} %copy-done.4, bf16[16,3,128,128]{3,2,1,0:T(8,128)(2,1)S(1)} %copy-done.4), custom_call_target="tpu_custom_call" | custom-call | flops 2147483648 | bytes 2097152 | tf_op jit(solution)/shard_map/pallas_call | solution.py:91
  127.8 7.6 %all-to-all-start.3 = ((bf16[16,128,128]{2,1,0:T(8,128)(2,1)}), bf16[16,128,128]{2,1,0:T(8,128)(2,1)}, u32[]{:S(2)}, u32[]{:S(2)}) async-start(bf16[16,128,128]{2,1,0:T(8,128)(2,1)} %shard_map.51), calls=%async_computation.3 | async-start | bytes 1048576 | tf_op jit(solution)/shard_map/all_to_all | solution.py:326
  140.8 2.7 %collective-permute-start.20 = (bf16[2,8,2,128,128]{4,3,2,1,0:T(8,128)(2,1)S(1)}, bf16[2,8,2,128,128]{4,3,2,1,0:T(8,128)(2,1)}, u32[]{:S(2)}, u32[]{:S(2)}) collective-permute-start(bf16[2,8,2,128,128]{4,3,2,1,0:T(8,128)(2,1)S(1)} %pad_maximum_fusion.2.refs_6_), channel_id=1, source_target_pairs={{0,96},{32,0},{64,32},{96,64},{1,97},{33,1},{65,33},{97,65},{2,98}... | collective-permute-start | bytes 3145736 | tf_op jit(solution)/shard_map/ppermute | solution.py:273
  144.9 6.2 %shard_map.47 = bf16[16,128,128]{2,1,0:T(8,128)(2,1)} custom-call(bf16[16,3,128,128]{3,2,1,0:T(8,128)(2,1)S(1)} %copy-done.2, bf16[16,3,128,128]{3,2,1,0:T(8,128)(2,1)S(1)} %copy-done.2, bf16[16,3,128,128]{3,2,1,0:T(8,128)(2,1)S(1)} %copy-done.2), custom_call_target="tpu_custom_call" | custom-call | flops 2147483648 | bytes 2097152 | tf_op jit(solution)/shard_map/pallas_call | solution.py:91
  151.1 8.7 %all-to-all-start.1 = ((bf16[16,128,128]{2,1,0:T(8,128)(2,1)}), bf16[16,128,128]{2,1,0:T(8,128)(2,1)}, u32[]{:S(2)}, u32[]{:S(2)}) async-start(bf16[16,128,128]{2,1,0:T(8,128)(2,1)} %shard_map.47), calls=%async_computation.1 | async-start | bytes 1048576 | tf_op jit(solution)/shard_map/all_to_all | solution.py:326
  162.7 18.9 %collective-permute-done.19.refs_9_ = bf16[2,8,2,128,128]{4,3,2,1,0:T(8,128)(2,1)} collective-permute-done((bf16[2,8,2,128,128]{4,3,2,1,0:T(8,128)(2,1)S(1)}, bf16[2,8,2,128,128]{4,3,2,1,0:T(8,128)(2,1)}, u32[]{:S(2)}, u32[]{:S(2)}) %collective-permute-start.19) | collective-permute-done | bytes 1048608 | tf_op jit(solution)/shard_map/ppermute | solution.py:273
  181.5 15.1 %collective-permute-start.23 = (bf16[16,128,128]{2,1,0:T(8,128)(2,1)}, bf16[16,128,128]{2,1,0:T(8,128)(2,1)}, u32[]{:S(2)}, u32[]{:S(2)}) collective-permute-start(bf16[16,128,128]{2,1,0:T(8,128)(2,1)} %all-to-all-done.3.refs_0_.a_ref), channel_id=1, source_target_pairs={{0,16},{16,0},{1,17},{17,1},{2,18},{18,2},{3,19},{19,3},{4,20},{20... | collective-permute-start | bytes 1572872 | tf_op jit(solution)/shard_map/ppermute | solution.py:285
  196.8 4.8 %collective-permute-done.21.refs_11_ = bf16[2,8,2,128,128]{4,3,2,1,0:T(8,128)(2,1)} collective-permute-done((bf16[2,8,2,128,128]{4,3,2,1,0:T(8,128)(2,1)}, bf16[2,8,2,128,128]{4,3,2,1,0:T(8,128)(2,1)}, u32[]{:S(2)}, u32[]{:S(2)}) %collective-permute-start.21) | collective-permute-done | bytes 1048608 | tf_op jit(solution)/shard_map/ppermute | solution.py:273
  201.6 2.6 %collective-permute-done.22.refs_12_ = bf16[2,8,2,128,128]{4,3,2,1,0:T(8,128)(2,1)} collective-permute-done((bf16[2,8,2,128,128]{4,3,2,1,0:T(8,128)(2,1)}, bf16[2,8,2,128,128]{4,3,2,1,0:T(8,128)(2,1)}, u32[]{:S(2)}, u32[]{:S(2)}) %collective-permute-start.22) | collective-permute-done | bytes 1048608 | tf_op jit(solution)/shard_map/ppermute | solution.py:273
  204.1 2.5 %shard_map.52 = (bf16[4,8,64,128]{3,2,1,0:T(8,128)(2,1)S(1)}, bf16[4,8,64,128]{3,2,1,0:T(8,128)(2,1)S(1)}, bf16[4,8,64,128]{3,2,1,0:T(8,128)(2,1)S(1)}, bf16[4,8...) custom-call(bf16[16,128,128]{2,1,0:T(8,128)(2,1)} %all-to-all-done.3, ...), custom_call_target="tpu_custom_call" | custom-call | bytes 8388608 | tf_op jit(solution)/shard_map/pallas_call | solution.py:151
  206.6 2.5 %shard_map.49 = (bf16[4,8,64,128]{3,2,1,0:T(8,128)(2,1)S(1)}, bf16[4,8,64,128]{3,2,1,0:T(8,128)(2,1)S(1)}, bf16[4,8,64,128]{3,2,1,0:T(8,128)(2,1)S(1)}, bf16[4,8...) custom-call(bf16[16,128,128]{2,1,0:T(8,128)(2,1)} %all-to-all-done.1, ...), custom_call_target="tpu_custom_call" | custom-call | bytes 8388608 | tf_op jit(solution)/shard_map/pallas_call | solution.py:151
  209.1 4.9 %shard_map.53.refs_12_ = f32[2,4,192,256]{3,2,1,0:T(8,128)} custom-call(s32[5]{0:T(128)S(1)} %stack.56.pos_ref, bf16[16,128,128]{2,1,0:T(8,128)(2,1)} %all-to-all-done.3.refs_0_.a_ref, bf16[16,128,128]{2,1,0:T(8,128)(2,1)} %collective-permute-done.23.b_ref, bf16[4,8,64,128]{3,2,1,0:T(8,128)(2,1)S(1)} %get-tuple-element.47.refs_0_, ...), custom_call_target="tpu_custom_call" | custom-call | flops 1610612736 | bytes 9437184 | tf_op jit(solution)/shard_map/pallas_call | solution.py:210
  215.4 3.7 %shard_map.54 = (bf16[2,4,192,128]{3,2,1,0:T(8,128)(2,1)S(1)}, bf16[2,4,192,128]{3,2,1,0:T(8,128)(2,1)S(1)}) custom-call(s32[5]{0:T(128)S(1)} %stack.56.pos_ref, bf16[16,128,128]{2,1,0:T(8,128)(2,1)} %all-to-all-done.1.refs_0_.a_ref, bf16[16,128,128]{2,1,0:T(8,128)(2,1)} %collective-permute-done.b_ref, ...), custom_call_target="tpu_custom_call" | custom-call | flops 1610612736 | bytes 9437184 | tf_op jit(solution)/shard_map/pallas_call | solution.py:210
  219.2 7.8 %collective-permute-start.24 = (bf16[2,4,192,128]{3,2,1,0:T(8,128)(2,1)S(1)}, bf16[2,4,192,128]{3,2,1,0:T(8,128)(2,1)S(1)}, u32[]{:S(2)}, u32[]{:S(2)}) collective-permute-start(bf16[2,4,192,128]{3,2,1,0:T(8,128)(2,1)S(1)} %get-tuple-element.60), channel_id=1, source_target_pairs={{0,16},{16,0},{1,17},{17,1},{2,18},{18,2},{3,19},{19,3},{4,20},{20... | collective-permute-start | bytes 1179656 | tf_op jit(solution)/shard_map/ppermute | solution.py:285
  (60 shorter events, 35.7 us)
Async XLA Ops:
  2.6 46.5 %all-to-all-start.2 = ((bf16[16,3,128,128]{3,2,1,0:T(8,128)(2,1)}), bf16[16,3,128,128]{3,2,1,0:T(8,128)(2,1)S(1)}, u32[]{:S(2)}, u32[]{:S(2)}) async-start(bf16[16,3,128,128]{3,2,1,0:T(8,128)(2,1)} %shard_map.50), calls=%async_computation.2 | async-start | bytes 3145728 | tf_op jit(solution)/shard_map/all_to_all | solution.py:326
  50.3 76.3 %all-to-all-start = ((bf16[16,3,128,128]{3,2,1,0:T(8,128)(2,1)}), bf16[16,3,128,128]{3,2,1,0:T(8,128)(2,1)S(1)}, u32[]{:S(2)}, u32[]{:S(2)}) async-start(bf16[16,3,128,128]{3,2,1,0:T(8,128)(2,1)} %shard_map.46), calls=%async_computation | async-start | bytes 3145728 | tf_op jit(solution)/shard_map/all_to_all | solution.py:326
  56.9 38.9 %collective-permute-start.3 = (bf16[192,256]{1,0:T(8,128)(2,1)S(1)}, bf16[192,256]{1,0:T(8,128)(2,1)S(1)}, u32[]{:S(2)}, u32[]{:S(2)}) collective-permute-start(bf16[192,256]{1,0:T(8,128)(2,1)S(1)} %bitcast.20), channel_id=1, source_target_pairs={{0,2},{1,3},{2,4},{3,5},{4,6},{5,7},{6,0},{7,1},{8,10},{9,11},{10,... | collective-permute-start | bytes 294920 | tf_op jit(solution)/shard_map/ppermute | solution.py:273
  59.3 40.5 %collective-permute-start.4 = (bf16[192,256]{1,0:T(8,128)(2,1)S(1)}, bf16[192,256]{1,0:T(8,128)(2,1)S(1)}, u32[]{:S(2)}, u32[]{:S(2)}) collective-permute-start(bf16[192,256]{1,0:T(8,128)(2,1)S(1)} %bitcast.21), channel_id=1, source_target_pairs={{0,6},{1,7},{2,0},{3,1},{4,2},{5,3},{6,4},{7,5},{8,14},{9,15},{10,... | collective-permute-start | bytes 294920 | tf_op jit(solution)/shard_map/ppermute | solution.py:273
  60.6 40.2 %collective-permute-start.1 = (bf16[192,256]{1,0:T(8,128)(2,1)S(1)}, bf16[192,256]{1,0:T(8,128)(2,1)S(1)}, u32[]{:S(2)}, u32[]{:S(2)}) collective-permute-start(bf16[192,256]{1,0:T(8,128)(2,1)S(1)} %bitcast.22), channel_id=1, source_target_pairs={{0,1},{1,2},{2,3},{3,4},{4,5},{5,6},{6,7},{7,0},{8,9},{9,10},{10,1... | collective-permute-start | bytes 294920 | tf_op jit(solution)/shard_map/ppermute | solution.py:273
  62.0 38.8 %collective-permute-start.2 = (bf16[192,256]{1,0:T(8,128)(2,1)S(1)}, bf16[192,256]{1,0:T(8,128)(2,1)S(1)}, u32[]{:S(2)}, u32[]{:S(2)}) collective-permute-start(bf16[192,256]{1,0:T(8,128)(2,1)S(1)} %bitcast.23), channel_id=1, source_target_pairs={{0,7},{1,0},{2,1},{3,2},{4,3},{5,4},{6,5},{7,6},{8,15},{9,8},{10,9... | collective-permute-start | bytes 294920 | tf_op jit(solution)/shard_map/ppermute | solution.py:273
  105.5 10.7 %collective-permute-start.14 = (bf16[8,2,128,128]{3,2,1,0:T(8,128)(2,1)S(1)}, bf16[8,2,128,128]{3,2,1,0:T(8,128)(2,1)}, u32[]{:S(2)}, u32[]{:S(2)}) collective-permute-start(bf16[8,2,128,128]{3,2,1,0:T(8,128)(2,1)S(1)} %get-tuple-element.34), channel_id=1, source_target_pairs={{0,8},{8,0},{1,9},{9,1},{2,10},{10,2},{3,11},{11,3},{4,12},{12,4},... | collective-permute-start | bytes 1572872 | tf_op jit(solution)/shard_map/ppermute | solution.py:277
  107.6 10.5 %collective-permute-start.9 = (bf16[8,2,64,128]{3,2,1,0:T(8,128)(2,1)S(1)}, bf16[8,2,64,128]{3,2,1,0:T(8,128)(2,1)S(1)}, u32[]{:S(2)}, u32[]{:S(2)}) collective-permute-start(bf16[8,2,64,128]{3,2,1,0:T(8,128)(2,1)S(1)} %get-tuple-element.33), channel_id=1, source_target_pairs={{0,96},{32,0},{64,32},{96,64},{1,97},{33,1},{65,33},{97,65},{2,98}... | collective-permute-start | bytes 786440 | tf_op jit(solution)/shard_map/ppermute | solution.py:273
  113.2 26.3 %collective-permute-start.15 = (bf16[8,2,128,128]{3,2,1,0:T(8,128)(2,1)S(1)}, bf16[8,2,128,128]{3,2,1,0:T(8,128)(2,1)}, u32[]{:S(2)}, u32[]{:S(2)}) collective-permute-start(bf16[8,2,128,128]{3,2,1,0:T(8,128)(2,1)S(1)} %get-tuple-element.34), channel_id=1, source_target_pairs={{8,128},{128,8},{136,0},{0,136},{9,129},{129,9},{137,1},{1,137},{1... | collective-permute-start | bytes 1572872 | tf_op jit(solution)/shard_map/ppermute | solution.py:281
  116.2 23.3 %collective-permute-start.16 = (bf16[8,2,128,128]{3,2,1,0:T(8,128)(2,1)}, bf16[8,2,128,128]{3,2,1,0:T(8,128)(2,1)}, u32[]{:S(2)}, u32[]{:S(2)}) collective-permute-start(bf16[8,2,128,128]{3,2,1,0:T(8,128)(2,1)} %collective-permute-done.14), channel_id=1, source_target_pairs={{8,128},{128,8},{136,0},{0,136},{9,129},{129,9},{137,1},{1,137},{1... | collective-permute-start | bytes 1572872 | tf_op jit(solution)/shard_map/ppermute | solution.py:281
  119.8 23.8 %collective-permute-start.11 = (bf16[4,8,2,64,128]{4,3,2,1,0:T(8,128)(2,1)S(1)}, bf16[4,8,2,64,128]{4,3,2,1,0:T(8,128)(2,1)}, u32[]{:S(2)}, u32[]{:S(2)}) collective-permute-start(bf16[4,8,2,64,128]{4,3,2,1,0:T(8,128)(2,1)S(1)} %pad_maximum_fusion.refs_1_), channel_id=1, source_target_pairs={{0,8},{8,0},{1,9},{9,1},{2,10},{10,2},{3,11},{11,3},{4,12},{12,4},... | collective-permute-start | bytes 3145736 | tf_op jit(solution)/shard_map/ppermute | solution.py:277
  127.8 23.3 %all-to-all-start.3 = ((bf16[16,128,128]{2,1,0:T(8,128)(2,1)}), bf16[16,128,128]{2,1,0:T(8,128)(2,1)}, u32[]{:S(2)}, u32[]{:S(2)}) async-start(bf16[16,128,128]{2,1,0:T(8,128)(2,1)} %shard_map.51), calls=%async_computation.3 | async-start | bytes 1048576 | tf_op jit(solution)/shard_map/all_to_all | solution.py:326
  136.5 23.4 %collective-permute-start.17 = (bf16[2,8,2,128,128]{4,3,2,1,0:T(8,128)(2,1)S(1)}, bf16[2,8,2,128,128]{4,3,2,1,0:T(8,128)(2,1)}, u32[]{:S(2)}, u32[]{:S(2)}) collective-permute-start(bf16[2,8,2,128,128]{4,3,2,1,0:T(8,128)(2,1)S(1)} %pad_maximum_fusion.1.refs_5_), channel_id=1, source_target_pairs={{0,32},{32,64},{64,96},{96,0},{1,33},{33,65},{65,97},{97,1},{2,34}... | collective-permute-start | bytes 3145736 | tf_op jit(solution)/shard_map/ppermute | solution.py:273
  137.6 22.2 %collective-permute-start.12 = (bf16[4,8,2,64,128]{4,3,2,1,0:T(8,128)(2,1)S(1)}, bf16[4,8,2,64,128]{4,3,2,1,0:T(8,128)(2,1)}, u32[]{:S(2)}, u32[]{:S(2)}) collective-permute-start(bf16[4,8,2,64,128]{4,3,2,1,0:T(8,128)(2,1)S(1)} %pad_maximum_fusion.refs_1_), channel_id=1, source_target_pairs={{8,128},{128,8},{136,0},{0,136},{9,129},{129,9},{137,1},{1,137},{1... | collective-permute-start | bytes 3145736 | tf_op jit(solution)/shard_map/ppermute | solution.py:281
  140.8 20.4 %collective-permute-start.20 = (bf16[2,8,2,128,128]{4,3,2,1,0:T(8,128)(2,1)S(1)}, bf16[2,8,2,128,128]{4,3,2,1,0:T(8,128)(2,1)}, u32[]{:S(2)}, u32[]{:S(2)}) collective-permute-start(bf16[2,8,2,128,128]{4,3,2,1,0:T(8,128)(2,1)S(1)} %pad_maximum_fusion.2.refs_6_), channel_id=1, source_target_pairs={{0,96},{32,0},{64,32},{96,64},{1,97},{33,1},{65,33},{97,65},{2,98}... | collective-permute-start | bytes 3145736 | tf_op jit(solution)/shard_map/ppermute | solution.py:273
  143.4 38.1 %collective-permute-start.19 = (bf16[2,8,2,128,128]{4,3,2,1,0:T(8,128)(2,1)S(1)}, bf16[2,8,2,128,128]{4,3,2,1,0:T(8,128)(2,1)}, u32[]{:S(2)}, u32[]{:S(2)}) collective-permute-start(bf16[2,8,2,128,128]{4,3,2,1,0:T(8,128)(2,1)S(1)} %pad_maximum_fusion.1.refs_5_), channel_id=1, source_target_pairs={{0,96},{32,0},{64,32},{96,64},{1,97},{33,1},{65,33},{97,65},{2,98}... | collective-permute-start | bytes 3145736 | tf_op jit(solution)/shard_map/ppermute | solution.py:273
  143.5 53.1 %collective-permute-start.18 = (bf16[2,8,2,128,128]{4,3,2,1,0:T(8,128)(2,1)S(1)}, bf16[2,8,2,128,128]{4,3,2,1,0:T(8,128)(2,1)}, u32[]{:S(2)}, u32[]{:S(2)}) collective-permute-start(bf16[2,8,2,128,128]{4,3,2,1,0:T(8,128)(2,1)S(1)} %pad_maximum_fusion.2.refs_6_), channel_id=1, source_target_pairs={{0,32},{32,64},{64,96},{96,0},{1,33},{33,65},{65,97},{97,1},{2,34}... | collective-permute-start | bytes 3145736 | tf_op jit(solution)/shard_map/ppermute | solution.py:273
  151.1 45.5 %all-to-all-start.1 = ((bf16[16,128,128]{2,1,0:T(8,128)(2,1)}), bf16[16,128,128]{2,1,0:T(8,128)(2,1)}, u32[]{:S(2)}, u32[]{:S(2)}) async-start(bf16[16,128,128]{2,1,0:T(8,128)(2,1)} %shard_map.47), calls=%async_computation.1 | async-start | bytes 1048576 | tf_op jit(solution)/shard_map/all_to_all | solution.py:326
  159.8 37.0 %collective-permute-start.13 = (bf16[4,8,2,64,128]{4,3,2,1,0:T(8,128)(2,1)}, bf16[4,8,2,64,128]{4,3,2,1,0:T(8,128)(2,1)}, u32[]{:S(2)}, u32[]{:S(2)}) collective-permute-start(bf16[4,8,2,64,128]{4,3,2,1,0:T(8,128)(2,1)} %collective-permute-done.11.refs_2_), channel_id=1, source_target_pairs={{8,128},{128,8},{136,0},{0,136},{9,129},{129,9},{137,1},{1,137},{1... | collective-permute-start | bytes 3145736 | tf_op jit(solution)/shard_map/ppermute | solution.py:281
  159.9 41.6 %collective-permute-start.21 = (bf16[2,8,2,128,128]{4,3,2,1,0:T(8,128)(2,1)}, bf16[2,8,2,128,128]{4,3,2,1,0:T(8,128)(2,1)}, u32[]{:S(2)}, u32[]{:S(2)}) collective-permute-start(bf16[2,8,2,128,128]{4,3,2,1,0:T(8,128)(2,1)} %collective-permute-done.17.refs_7_), channel_id=1, source_target_pairs={{0,32},{32,64},{64,96},{96,0},{1,33},{33,65},{65,97},{97,1},{2,34}... | collective-permute-start | bytes 3145736 | tf_op jit(solution)/shard_map/ppermute | solution.py:273
  161.2 42.9 %collective-permute-start.22 = (bf16[2,8,2,128,128]{4,3,2,1,0:T(8,128)(2,1)}, bf16[2,8,2,128,128]{4,3,2,1,0:T(8,128)(2,1)}, u32[]{:S(2)}, u32[]{:S(2)}) collective-permute-start(bf16[2,8,2,128,128]{4,3,2,1,0:T(8,128)(2,1)} %collective-permute-done.20.refs_10_), channel_id=1, source_target_pairs={{0,96},{32,0},{64,32},{96,64},{1,97},{33,1},{65,33},{97,65},{2,98}... | collective-permute-start | bytes 3145736 | tf_op jit(solution)/shard_map/ppermute | solution.py:273
  181.5 27.6 %collective-permute-start.23 = (bf16[16,128,128]{2,1,0:T(8,128)(2,1)}, bf16[16,128,128]{2,1,0:T(8,128)(2,1)}, u32[]{:S(2)}, u32[]{:S(2)}) collective-permute-start(bf16[16,128,128]{2,1,0:T(8,128)(2,1)} %all-to-all-done.3.refs_0_.a_ref), channel_id=1, source_target_pairs={{0,16},{16,0},{1,17},{17,1},{2,18},{18,2},{3,19},{19,3},{4,20},{20... | collective-permute-start | bytes 1572872 | tf_op jit(solution)/shard_map/ppermute | solution.py:285
  196.6 17.4 %collective-permute-start = (bf16[16,128,128]{2,1,0:T(8,128)(2,1)}, bf16[16,128,128]{2,1,0:T(8,128)(2,1)}, u32[]{:S(2)}, u32[]{:S(2)}) collective-permute-start(bf16[16,128,128]{2,1,0:T(8,128)(2,1)} %all-to-all-done.1.refs_0_.a_ref), channel_id=1, source_target_pairs={{0,16},{16,0},{1,17},{17,1},{2,18},{18,2},{3,19},{19,3},{4,20},{20... | collective-permute-start | bytes 1572872 | tf_op jit(solution)/shard_map/ppermute | solution.py:285
  219.2 9.2 %collective-permute-start.24 = (bf16[2,4,192,128]{3,2,1,0:T(8,128)(2,1)S(1)}, bf16[2,4,192,128]{3,2,1,0:T(8,128)(2,1)S(1)}, u32[]{:S(2)}, u32[]{:S(2)}) collective-permute-start(bf16[2,4,192,128]{3,2,1,0:T(8,128)(2,1)S(1)} %get-tuple-element.60), channel_id=1, source_target_pairs={{0,16},{16,0},{1,17},{17,1},{2,18},{18,2},{3,19},{19,3},{4,20},{20... | collective-permute-start | bytes 1179656 | tf_op jit(solution)/shard_map/ppermute | solution.py:285
  (11 other events, 148.8 us)
